TPU v7x, 256 devices: a whole 4x4x8 slice. The times are simulated.
256 devices in a mesh: region: 4 (over x_hi, core), shard: 64 (over y, x_lo, z).
Axes of the slice: x: 4 (x_hi: 2, x_lo: 2; x = x_hi * 2 + x_lo), y: 4, z: 8, core: 2. Of those that a mesh axis runs over, the one named last changes fastest.
Arguments:
- region_role: int32 [4], replicated, may hold values from 0 to 3, each once
- tokens: bfloat16 [8192, 5120], P(('region', 'shard')), may hold values from -6 to 6
- cotangent: bfloat16 [8192, 16384], P('region', 'shard'), may hold values from -0.125 to 0.125
- master: float32 [5120, 16384], P('region', 'shard'), may hold values from -3 to 3
- momentum: float32 [5120, 16384], P('region', 'shard'), may hold values from -6 to 6
Outputs:
- new_master: float32 [5120, 16384], P('region', 'shard')
- new_momentum: float32 [5120, 16384], P('region', 'shard')
- learner_weight: bfloat16 [5120, 16384], P(None, 'shard')
- rollout_weight: bfloat16 [4, 1280, 16384], P(None, 'shard')
Inputs may be any that keep to these rules, and one draw needn't show every extreme that they name: `region_role`: the two regions holding 0 and 1 form the larger learner group, the region holding 2 is the smaller learner group, the region holding 3 serves rollout; each value appears once.
All inputs are finite; a program needn't handle non-finite values.
Results may differ from a plain program's by a relative error of at most 0.001.
Values may be sent and summed in bfloat16 or wider, within the bound.
No kernel may reach another device: no remote copies, remote signals or barrier semaphores. Data moves between devices by JAX's collectives and lax.ppermute only.
A program may use at most 128 MiB of HBM per device.

v0:
```python
import jax
import jax.numpy as jnp
from jax import lax
from jax.sharding import PartitionSpec as P


def per_device(region_role, tokens, cotangent, master, momentum):
    here = lax.axis_index("region")
    role = region_role[here]
    share = jnp.where(role < 2, 0.25, jnp.where(role == 2, 0.5, 0.0)).astype(jnp.float32)
    columns = cotangent.shape[1]
    grad = lax.dot_general(
        lax.all_gather(tokens, "shard", axis=0, tiled=True),
        cotangent,
        (((0,), (0,)), ((), ())),
        preferred_element_type=jnp.float32,
    )
    delta = lax.psum_scatter(share * grad, "region", scatter_dimension=0, tiled=True)
    new_momentum = 0.9 * momentum + delta
    new_master = master - 0.7 * (delta + 0.9 * new_momentum)
    fresh = new_master.astype(jnp.bfloat16)
    learner_weight = lax.all_gather(fresh, "region", axis=0, tiled=True)
    blocks = learner_weight.reshape(lax.axis_size("region"), fresh.shape[0], columns)
    rollout_weight = lax.all_to_all(blocks, "shard", split_axis=1, concat_axis=2, tiled=True)
    return (new_master, new_momentum, learner_weight, rollout_weight)


def solution(mesh):
    in_specs = (
        P(),
        P(("region", "shard"), None),
        P("region", "shard"),
        P("region", "shard"),
        P("region", "shard"),
    )
    out_specs = (
        P("region", "shard"),
        P("region", "shard"),
        P(None, "shard"),
        P(None, "shard", None),
    )
    return jax.shard_map(
        per_device, mesh=mesh, in_specs=in_specs, out_specs=out_specs, check_vma=False
    )
```

profile of v0, /device:TPU:1, one launch (start us, length us, event | category | flops | bytes accessed | tf_op | source)
XLA Modules:
  0.0 553.8 jit_solution(7032518835989908348)
XLA Ops:
  7.2 0.0 copy-start
  7.2 0.0 all-gather.3.cloned.1.call-start
  7.2 0.7 all-gather.3.cloned.1.call-update
  7.9 0.0 reduce-scatter.2.cloned.1.call-start
  8.0 1.2 dynamic_slice.3
  10.5 304.2 %all-gather.3.cloned.1.call-done = bf16[2048,5120]{1,0:T(8,128)(2,1)} async-done(((bf16[32,5120]{1,0:T(8,128)(2,1)}), bf16[2048,5120]{1,0:T(8,128)(2,1)}) %all-gather.3.cloned.1.call-update) | async-done | bytes 20971536 | tf_op jit(solution)/shard_map/all_gather | solution.py:13
  314.7 0.0 copy-done
  314.7 12.7 %convolution_multiply_fusion = f32[5120,256]{1,0:T(8,128)} fusion(bf16[2048,5120]{1,0:T(8,128)(2,1)} %all-gather.3.cloned.1.call-done, bf16[2048,256]{1,0:T(8,128)(2,1)S(1)} %copy-done, f32[]{:T(128)} %bitcast), kind=kOutput, calls=%fused_computation | convolution fusion | flops 5370019840 | bytes 27262980 | tf_op jit(solution)/shard_map/dot_general | solution.py:12
  327.4 0.0 copy-start.2
  327.4 0.0 reduce-scatter.2.cloned.1.call-update
  327.4 0.0 all-gather.5.cloned.1.call-start
  327.5 96.6 %reduce-scatter.2.cloned.1.call-done = f32[1280,256]{1,0:T(8,128)} async-done(((f32[5120,256]{1,0:T(8,128)}), f32[1280,256]{1,0:T(8,128)}) %reduce-scatter.2.cloned.1.call-update) | async-done | bytes 1310736 | tf_op jit(solution)/shard_map/reduce_scatter | solution.py:18
  424.1 0.0 copy-done.2
  424.1 3.7 fusion
  427.8 0.0 all-gather.5.cloned.1.call-update
  427.8 32.2 %all-gather.5.cloned.1.call-done = bf16[5120,256]{1,0:T(8,128)(2,1)} async-done(((bf16[1280,256]{1,0:T(8,128)(2,1)}), bf16[5120,256]{1,0:T(8,128)(2,1)}) %all-gather.5.cloned.1.call-update) | async-done | bytes 2621456 | tf_op jit(solution)/shard_map/all_gather | solution.py:22
  460.0 11.1 %copy.11 = bf16[4,1280,256]{2,0,1:T(4,128)(2,1)S(1)} copy(bf16[4,1280,256]{2,1,0:T(8,128)(2,1)} %bitcast.9) | data formatting | bytes 5242880 | tf_op jit(solution)/shard_map/reshape | solution.py:23
  471.1 71.9 %all_to_all.18 = bf16[4,1280,256]{2,0,1:T(4,128)(2,1)S(1)} all-to-all(bf16[4,1280,256]{2,0,1:T(4,128)(2,1)S(1)} %copy.11), channel_id=1, replica_groups=mesh['region'=4,'shard'=64] {'shard'}, dimensions={1} | all-to-all | bytes 5242880 | tf_op jit(solution)/shard_map/all_to_all | solution.py:24
  543.0 0.0 copy-start.1
  543.0 2.8 copy.13
  545.8 0.0 copy-done.1
  545.8 1.5 copy.15
Async XLA Ops:
  7.2 307.6 %copy-start = (bf16[2048,256]{1,0:T(8,128)(2,1)S(1)}, bf16[2048,256]{1,0:T(8,128)(2,1)}, u32[]{:S(2)}) copy-start(bf16[2048,256]{1,0:T(8,128)(2,1)} %param.7) | copy-start | bytes 3145732
  7.2 307.6 %all-gather.3.cloned.1.call-start = ((), (), s32[]{:S(2)}) async-start(), calls=%async_computation.2 | async-start | bytes 21299200 | tf_op jit(solution)/shard_map/all_gather | solution.py:13
  7.9 416.1 %reduce-scatter.2.cloned.1.call-start = ((), (), s32[]{:S(2)}) async-start(), calls=%async_computation.3 | async-start | bytes 6553600 | tf_op jit(solution)/shard_map/reduce_scatter | solution.py:18
  327.4 96.6 %copy-start.2 = (f32[1280,256]{1,0:T(8,128)S(1)}, f32[1280,256]{1,0:T(8,128)}, u32[]{:S(2)}) copy-start(f32[1280,256]{1,0:T(8,128)} %param.8) | copy-start | bytes 3932164
  327.4 132.6 %all-gather.5.cloned.1.call-start = ((), (), s32[]{:S(2)}) async-start(), calls=%async_computation.4 | async-start | bytes 3276800 | tf_op jit(solution)/shard_map/all_gather | solution.py:22
  543.0 2.8 copy-start.1
Sparse Core Ops, SparseCore 0:
  9.8 304.8 all-gather.2
  327.6 96.4 reduce-scatter.1
  428.0 32.0 all-gather.4
where the time goes:
time: 555 us; the launch traced here: 554 us
  waiting for transfers between devices  434 us (78%)
  blocking collectives  71.9 us (13%)
  local copies, waits for them, and re-layouts  16.7 us (3%)
  between operations  15.1 us (3%)
  matrix products  12.7 us (2%)
    all_gather x1, waiting for transfers between devices, per_device(): lax.all_gather(tokens, 'shard', axis=0, tiled=True)  304 us
    reduce_scatter x1, waiting for transfers between devices, per_device(): lax.psum_scatter(share * grad, 'region', scatter_dimension=0, tiled=True)  96.6 us
    all_to_all x1, blocking collectives, per_device(): lax.all_to_all(blocks, 'shard', split_axis=1, concat_axis=2, tiled=True)  71.9 us
    all_gather x1, waiting for transfers between devices, per_device(): learner_weight = lax.all_gather(fresh, 'region', axis=0, tiled=True)  32.2 us
    dot_general x1, matrix products, per_device(): lax.dot_general(lax.all_gather(tokens, 'shard', axis=0, tiled=True), cota...  12.7 us
    reshape x1, local copies, waits for them, and re-layouts, per_device(): learner_weight.reshape(lax.axis_size('region'), fresh.shape[0], columns)  11.1 us
  transfers between devices with their start and end apart: 3, of which 3 were waited for; matrix products, arithmetic and copies ran while one was open for 0% of the time, Pallas kernels for 0%

commit v1 on v0

v1 whole, which is shorter than its diff:
```python
import functools

import jax
import jax.numpy as jnp
from jax import lax
from jax.experimental import pallas as pl
from jax.experimental.pallas import tpu as pltpu
from jax.sharding import Mesh, PartitionSpec as P

REGION = ("xh", "core")
SHARD = ("y", "xl", "z")
WIDE = 384


def shift(x, axis, n, by):
    return lax.ppermute(x, axis, [(i, (i + by) % n) for i in range(n)])


def ring(x, axis, n, half_axis):
    out = [None] * n
    out[0] = up = down = x
    for k in range(1, n // 2):
        up, down = shift(up, axis, n, 1), shift(down, axis, n, -1)
        out[n - k], out[k] = up, down
    half = x.shape[half_axis] // 2
    far = (
        shift(lax.slice_in_dim(up, 0, half, axis=half_axis), axis, n, 1),
        shift(lax.slice_in_dim(down, half, 2 * half, axis=half_axis), axis, n, -1),
    )
    out[n // 2] = jnp.concatenate(far, half_axis)
    return out


def gradient_kernel(ny, nz, *refs):
    wide, narrow, cot = refs[:ny], refs[ny : ny + nz], refs[ny + nz]
    own, other = refs[ny + nz + 1 :]
    mine = lax.axis_index("xl")
    for out, column in ((own, mine), (other, 1 - mine)):
        first = True
        for j in range(ny):
            for r in range(4):
                part = lax.dot_general(
                    wide[j][r], cot[2 * r + column, j].reshape(512, 256), (((0,), (0,)), ((), ())),
                    preferred_element_type=jnp.float32)
                if first:
                    out[:WIDE, :] = part
                    first = False
                else:
                    out[:WIDE, :] += part
        first = True
        for m in range(nz):
            for r in range(4):
                rows = jnp.concatenate(
                    [cot[2 * r + column, j, l, m] for j in range(ny) for l in range(2)], 0)
                part = lax.dot_general(
                    narrow[m][r], rows, (((0,), (0,)), ((), ())), preferred_element_type=jnp.float32)
                if first:
                    out[WIDE:, :] = part
                    first = False
                else:
                    out[WIDE:, :] += part


def gradient(wide, narrow, cot):
    ny, nz = len(wide), len(narrow)
    tile = jax.ShapeDtypeStruct((640, 256), jnp.float32)
    return pl.pallas_call(
        functools.partial(gradient_kernel, ny, nz),
        out_shape=(tile, tile),
        in_specs=[pl.BlockSpec(memory_space=pltpu.VMEM)] * (ny + nz + 1),
        out_specs=[pl.BlockSpec(memory_space=pltpu.VMEM)] * 2,
        compiler_params=pltpu.CompilerParams(vmem_limit_bytes=40 << 20),
        cost_estimate=pl.CostEstimate(flops=2 * 8192 * 640 * 512, bytes_accessed=20 << 20, transcendentals=0),
        name="gradient",
    )(*wide, *narrow, cot)


def roll_to(x, axis, start):
    return lax.dynamic_slice_in_dim(jnp.concatenate([x, x], axis), start, x.shape[axis], axis)


def per_device(region_role, tokens, cotangent, master, momentum):
    role = region_role[lax.axis_index(REGION)]
    share = jnp.where(role < 2, 0.25, jnp.where(role == 2, 0.5, 0.0)).astype(tokens.dtype)
    y, z, low = lax.axis_index("y"), lax.axis_index("z"), lax.axis_index("xl")

    cot = cotangent.reshape(4, 2, 8, 32, 256)
    cot = roll_to(roll_to(cot, 0, y), 2, z)
    cots = lax.all_gather(cot.reshape(2048, 256), ("xh", "core", "xl"), axis=0, tiled=True)
    cots = cots.reshape(8, 4, 2, 8, 32, 256)

    blocks = (tokens * share).reshape(32, 8, 640).transpose(1, 0, 2)
    here = lax.all_to_all(blocks, ("xh", "core", "xl"), split_axis=0, concat_axis=0, tiled=True)
    wide = [t[:, None] for t in ring(here[:, :, :WIDE], "z", 8, 1)]
    wide = jnp.concatenate(wide, 1)
    narrow = [t.reshape(4, 1, 2, 32, 640 - WIDE) for t in ring(here[:, :, WIDE:], "y", 4, 1)]
    narrow = jnp.concatenate(narrow, 1)
    wide = [t.reshape(4, 512, WIDE) for t in ring(wide, "y", 4, 0)]
    narrow = [t.reshape(4, 256, 640 - WIDE) for t in ring(narrow, "z", 8, 0)]

    own, other = gradient(wide, narrow, cots)
    came = shift(other, "xl", 2, 1)
    delta = jnp.where(low == 0, jnp.concatenate([own, came], 0), jnp.concatenate([came, own], 0))

    new_momentum = 0.9 * momentum + delta
    new_master = master - 0.7 * (delta + 0.9 * new_momentum)
    fresh = new_master.astype(jnp.bfloat16)
    learner_weight = lax.all_gather(fresh, REGION, axis=0, tiled=True)
    rows = lax.all_to_all(fresh.reshape(64, 20, 256), SHARD, split_axis=0, concat_axis=0, tiled=True)
    rows = rows.transpose(1, 0, 2).reshape(20, 16384)
    rollout_weight = lax.all_gather(rows, REGION, axis=0, tiled=False)
    return new_master, new_momentum, learner_weight, rollout_weight


def solution(mesh):
    fine = Mesh(mesh.devices.reshape(2, 2, 4, 2, 8), REGION + SHARD)
    tile = P(REGION, SHARD)
    return jax.shard_map(
        per_device,
        mesh=fine,
        in_specs=(P(), P(REGION + SHARD, None), tile, tile, tile),
        out_specs=(tile, tile, P(None, SHARD), P(None, SHARD, None)),
        check_vma=False,
    )
```

time: 555 us -> 275 us (0.50)
  waiting for transfers between devices: 434 us -> 137 us
  starting transfers between devices: 0.12 us -> 40 us
  blocking collectives: 71.9 us -> 41.8 us
  matrix products: 12.7 us -> 0 us
  Pallas kernels: 0 us -> 9.85 us
  local copies, waits for them, and re-layouts: 16.7 us -> 22.7 us
    all_gather x2 -> x3, waiting for transfers between devices: 336 us -> 57.4 us  [the longest x1 36.1 us: per_device(): rollout_weight = lax.all_gather(rows, REGION, axis=0, tiled=False)]
    reduce_scatter x1 -> x0, waiting for transfers between devices: 96.6 us -> none  [per_device(): lax.psum_scatter(share * grad, 'region', scatter_dimension=0, tiled=True)]
    ppermute x0 -> x25, waiting for transfers between devices: none -> 79.9 us  [shift(): return lax.ppermute(x, axis, [(i, (i + by) % n) for i in range(n)])]
    ppermute x0 -> x25, starting transfers between devices: none -> 39.9 us  [shift(): return lax.ppermute(x, axis, [(i, (i + by) % n) for i in range(n)])]
    all_to_all x1 -> x2, blocking collectives: 71.9 us -> 41.8 us  [the longest x1 28.6 us: per_device(): lax.all_to_all(fresh.reshape(64, 20, 256), SHARD, split_axis=0, concat_ax...]
    unnamed x7 -> x50, local copies, waits for them, and re-layouts: 1.51 us -> 19.2 us
    dot_general x1 -> x0, matrix products: 12.7 us -> none  [per_device(): lax.dot_general(lax.all_gather(tokens, 'shard', axis=0, tiled=True), cota...]
    reshape x1 -> x2, local copies, waits for them, and re-layouts: 11.1 us -> 1.25 us  [the longest x1 1.22 us: per_device(): fresh.reshape(64, 20, 256)]
  transfers between devices with their start and end apart: 3 -> 28, of which waited for: 3 -> 15; matrix products, arithmetic and copies ran while one was open for 0% -> 1% of each run, Pallas kernels for 0% -> 0%
where the time goes in v1:
time: 275 us; the launch traced here: 274 us
  waiting for transfers between devices  137 us (50%)
  blocking collectives  41.8 us (15%)
  starting transfers between devices  40 us (15%)
  local copies, waits for them, and re-layouts  22.7 us (8%)
  between operations  15.4 us (6%)
  Pallas kernels  9.85 us (4%)
  other arithmetic  7.14 us (3%)
    ppermute x25, waiting for transfers between devices, shift(): return lax.ppermute(x, axis, [(i, (i + by) % n) for i in range(n)])  79.9 us
    ppermute x25, starting transfers between devices, shift(): return lax.ppermute(x, axis, [(i, (i + by) % n) for i in range(n)])  39.9 us
    all_gather x1, waiting for transfers between devices, per_device(): rollout_weight = lax.all_gather(rows, REGION, axis=0, tiled=False)  36.1 us
    all_to_all x1, blocking collectives, per_device(): lax.all_to_all(fresh.reshape(64, 20, 256), SHARD, split_axis=0, concat_ax...  28.6 us
    unnamed x50, local copies, waits for them, and re-layouts  19.2 us
    all_to_all x1, blocking collectives, per_device(): lax.all_to_all(blocks, ('xh', 'core', 'xl'), split_axis=0, concat_axis=0,...  13.1 us
    all_gather x1, waiting for transfers between devices, per_device(): lax.all_gather(cot.reshape(2048, 256), ('xh', 'core', 'xl'), axis=0, tile...  10.8 us
    all_gather x1, waiting for transfers between devices, per_device(): learner_weight = lax.all_gather(fresh, REGION, axis=0, tiled=True)  10.4 us
  transfers between devices with their start and end apart: 28, of which 15 were waited for; matrix products, arithmetic and copies ran while one was open for 1% of the time, Pallas kernels for 0%

profile of v1, /device:TPU:1, one launch (start us, length us, event | category | flops | bytes accessed | tf_op | source)
XLA Modules:
  0.0 274.2 jit_solution(4619923009148714997)
XLA Ops:
  7.2 0.0 all-gather.4.cloned.1.call-start
  7.2 1.6 fusion.1
  8.9 1.4 fusion
  10.2 0.0 all-gather.6.cloned.1.call-start
  10.3 0.6 dynamic_slice.9
  12.3 13.1 %all_to_all.10 = bf16[8,32,640]{2,1,0:T(8,128)(2,1)S(1)} all-to-all(bf16[8,32,640]{2,1,0:T(8,128)(2,1)S(1)} %bitcast.75), channel_id=1, replica_groups=mesh['xh'=2,'core'=2,'y'=4,'xl'=2,'z'=8] {'xh','core','xl'}, dimensions={0} | all-to-all | bytes 655360 | tf_op jit(solution)/shard_map/all_to_all | solution.py:93
  25.4 5.6 %collective-permute-start = (bf16[8,32,384]{2,1,0:T(8,128)(2,1)S(1)}, bf16[8,32,384]{2,1,0:T(8,128)(2,1)S(1)}, u32[]{:S(2)}, u32[]{:S(2)}) collective-permute-start(bf16[8,32,384]{2,1,0:T(8,128)(2,1)S(1)} %slice.40), channel_id=1, source_target_pairs={{0,7},{1,0},{2,1},{3,2},{4,3},{5,4},{6,5},{7,6},{8,15},{9,8},{10,9... | collective-permute-start | bytes 589832 | tf_op jit(solution)/shard_map/ppermute | solution.py:16
  31.1 1.3 collective-permute-start.13
  32.4 1.6 collective-permute-start.12
  34.0 0.5 collective-permute-done
  34.6 3.5 %collective-permute-start.1 = (bf16[8,32,384]{2,1,0:T(8,128)(2,1)S(1)}, bf16[8,32,384]{2,1,0:T(8,128)(2,1)S(1)}, u32[]{:S(2)}, u32[]{:S(2)}) collective-permute-start(bf16[8,32,384]{2,1,0:T(8,128)(2,1)S(1)} %collective-permute-done), channel_id=1, source_target_pairs={{0,7},{1,0},{2,1},{3,2},{4,3},{5,4},{6,5},{7,6},{8,15},{9,8},{10,9... | collective-permute-start | bytes 589832 | tf_op jit(solution)/shard_map/ppermute | solution.py:16
  38.1 2.6 collective-permute-done.1
  40.7 3.5 %collective-permute-start.2 = (bf16[8,32,384]{2,1,0:T(8,128)(2,1)S(1)}, bf16[8,32,384]{2,1,0:T(8,128)(2,1)S(1)}, u32[]{:S(2)}, u32[]{:S(2)}) collective-permute-start(bf16[8,32,384]{2,1,0:T(8,128)(2,1)S(1)} %collective-permute-done.1), channel_id=1, source_target_pairs={{0,7},{1,0},{2,1},{3,2},{4,3},{5,4},{6,5},{7,6},{8,15},{9,8},{10,9... | collective-permute-start | bytes 589832 | tf_op jit(solution)/shard_map/ppermute | solution.py:16
  44.2 5.7 %collective-permute-done.5 = bf16[8,32,384]{2,1,0:T(8,128)(2,1)S(1)} collective-permute-done((bf16[8,32,384]{2,1,0:T(8,128)(2,1)S(1)}, bf16[8,32,384]{2,1,0:T(8,128)(2,1)S(1)}, u32[]{:S(2)}, u32[]{:S(2)}) %collective-permute-start.5) | collective-permute-done | bytes 196640 | tf_op jit(solution)/shard_map/ppermute | solution.py:16
  49.9 0.1 collective-permute-start.6
  50.0 2.7 collective-permute-start.7
  52.8 2.3 collective-permute-done.6
  55.2 1.3 collective-permute-start.9
  56.6 2.0 collective-permute-start.8
  58.5 0.1 collective-permute-start.14
  58.7 2.9 %collective-permute-start.15 = (bf16[8,16,256]{2,1,0:T(8,128)(2,1)S(1)}, bf16[8,16,256]{2,1,0:T(8,128)(2,1)S(1)}, u32[]{:S(2)}, u32[]{:S(2)}) collective-permute-start(bf16[8,16,256]{2,1,0:T(8,128)(2,1)S(1)} %slice.47), channel_id=1, source_target_pairs={{0,48},{16,0},{32,16},{48,32},{1,49},{17,1},{33,17},{49,33},{2,50}... | collective-permute-start | bytes 196616 | tf_op jit(solution)/shard_map/ppermute | solution.py:16
  61.6 28.5 %collective-permute-done.14 = bf16[8,16,256]{2,1,0:T(8,128)(2,1)S(1)} collective-permute-done((bf16[8,16,256]{2,1,0:T(8,128)(2,1)S(1)}, bf16[8,16,256]{2,1,0:T(8,128)(2,1)S(1)}, u32[]{:S(2)}, u32[]{:S(2)}) %collective-permute-start.14) | collective-permute-done | bytes 65568 | tf_op jit(solution)/shard_map/ppermute | solution.py:16
  90.1 0.1 pad_maximum_fusion.1
  90.2 0.1 collective-permute-start.19
  90.3 2.7 collective-permute-start.16
  92.9 6.6 %collective-permute-done.19 = bf16[4,4,2,32,256]{4,3,2,1,0:T(8,128)(2,1)S(1)} collective-permute-done((bf16[4,4,2,32,256]{4,3,2,1,0:T(8,128)(2,1)S(1)}, bf16[4,4,2,32,256]{4,3,2,1,0:T(8,128)(2,1)S(1)}, u32[]{:S(2)}, u32[]{:S(2)}) %collective-permute-start.19) | collective-permute-done | bytes 524320 | tf_op jit(solution)/shard_map/ppermute | solution.py:16
  99.5 0.8 copy-done.10
  100.3 2.7 collective-permute-start.17
  103.0 0.8 copy-done.12
  103.8 7.2 %collective-permute-done.20 = bf16[4,4,2,32,256]{4,3,2,1,0:T(8,128)(2,1)S(1)} collective-permute-done((bf16[4,4,2,32,256]{4,3,2,1,0:T(8,128)(2,1)S(1)}, bf16[4,4,2,32,256]{4,3,2,1,0:T(8,128)(2,1)S(1)}, u32[]{:S(2)}, u32[]{:S(2)}) %collective-permute-start.20) | collective-permute-done | bytes 524320 | tf_op jit(solution)/shard_map/ppermute | solution.py:16
  110.9 2.8 %collective-permute-start.18 = (bf16[4,4,2,32,256]{4,3,2,1,0:T(8,128)(2,1)S(1)}, bf16[4,4,2,32,256]{4,3,2,1,0:T(8,128)(2,1)S(1)}, u32[]{:S(2)}, u32[]{:S(2)}) collective-permute-start(bf16[4,4,2,32,256]{4,3,2,1,0:T(8,128)(2,1)S(1)} %collective-permute-done.17), channel_id=1, source_target_pairs={{0,7},{1,0},{2,1},{3,2},{4,3},{5,4},{6,5},{7,6},{8,15},{9,8},{10,9... | collective-permute-start | bytes 1572872 | tf_op jit(solution)/shard_map/ppermute | solution.py:16
  113.8 0.1 slice.43
  113.9 1.5 collective-permute-start.10
  115.4 0.1 slice.44
  115.5 2.1 collective-permute-start.11
  117.6 5.9 %collective-permute-done.21 = bf16[4,4,2,32,256]{4,3,2,1,0:T(8,128)(2,1)S(1)} collective-permute-done((bf16[4,4,2,32,256]{4,3,2,1,0:T(8,128)(2,1)S(1)}, bf16[4,4,2,32,256]{4,3,2,1,0:T(8,128)(2,1)S(1)}, u32[]{:S(2)}, u32[]{:S(2)}) %collective-permute-start.21) | collective-permute-done | bytes 524320 | tf_op jit(solution)/shard_map/ppermute | solution.py:16
  123.5 0.1 collective-permute-start.22
  123.6 0.1 collective-permute-done.18
  123.7 3.4 %collective-permute-start.23 = (bf16[2,4,2,32,256]{4,3,2,1,0:T(8,128)(2,1)S(1)}, bf16[2,4,2,32,256]{4,3,2,1,0:T(8,128)(2,1)S(1)}, u32[]{:S(2)}, u32[]{:S(2)}) collective-permute-start(bf16[2,4,2,32,256]{4,3,2,1,0:T(8,128)(2,1)S(1)} %slice.49), channel_id=1, source_target_pairs={{0,7},{1,0},{2,1},{3,2},{4,3},{5,4},{6,5},{7,6},{8,15},{9,8},{10,9... | collective-permute-start | bytes 786440 | tf_op jit(solution)/shard_map/ppermute | solution.py:16
  127.1 6.0 %collective-permute-done.22 = bf16[2,4,2,32,256]{4,3,2,1,0:T(8,128)(2,1)S(1)} collective-permute-done((bf16[2,4,2,32,256]{4,3,2,1,0:T(8,128)(2,1)S(1)}, bf16[2,4,2,32,256]{4,3,2,1,0:T(8,128)(2,1)S(1)}, u32[]{:S(2)}, u32[]{:S(2)}) %collective-permute-start.22) | collective-permute-done | bytes 262176 | tf_op jit(solution)/shard_map/ppermute | solution.py:16
  133.2 0.1 collective-permute-done.23
  133.4 0.2 pad_maximum_fusion
  133.6 10.8 %all-gather.4.cloned.1.call-done = bf16[16384,256]{1,0:T(8,128)(2,1)} async-done(((bf16[2048,256]{1,0:T(8,128)(2,1)}), bf16[16384,256]{1,0:T(8,128)(2,1)}) %all-gather.4.cloned.1.call-update) | async-done | bytes 8388624 | tf_op jit(solution)/shard_map/all_gather | solution.py:89
  144.4 1.4 copy-done.1
  145.8 1.4 copy-done.3
  147.2 1.0 copy-done.5
  148.2 1.0 copy-done.7
  149.3 1.4 copy-done.9
  150.7 1.0 copy-done.11
  151.7 1.0 copy-done.13
  152.8 1.0 copy-done.15
  153.8 1.0 copy-done.17
  154.8 9.8 %gradient.1 = (f32[640,256]{1,0:T(8,128)S(1)}, f32[640,256]{1,0:T(8,128)}) custom-call(bf16[4,512,384]{2,1,0:T(8,128)(2,1)S(1)} %bitcast.67, bf16[4,512,384]{2,1,0:T(8,128)(2,1)S(1)} %bitcast.64, bf16[4,512,384]{2,1,0:T(8,128)(2,1)S(1)} %bitcast.60, bf16[4,512,384]{2,1,0:T(8,128)(2,1)S(1)} %bitcast.63, bf16[4,256,256]{2,1,0:T(8,128)(2,1)S(1)} %bitcast.61, ...), custom_call_target="tpu_custom_call" | custom-call | flops 5368709120 | bytes 20971520 | tf_op jit(solution)/shard_map/gradient/pallas_call | solution.py:67
  164.7 14.4 %collective-permute-done.24 = f32[640,256]{1,0:T(8,128)S(1)} collective-permute-done((f32[640,256]{1,0:T(8,128)}, f32[640,256]{1,0:T(8,128)S(1)}, u32[]{:S(2)}, u32[]{:S(2)}) %collective-permute-start.24) | collective-permute-done | bytes 655392 | tf_op jit(solution)/shard_map/ppermute | solution.py:16
  179.1 3.8 %fusion.3 = (bf16[1280,256]{1,0:T(8,128)(2,1)}, f32[1280,256]{1,0:T(8,128)}, f32[1280,256]{1,0:T(8,128)}) fusion(f32[1280,256]{1,0:T(8,128)} %param.8, f32[640,256]{1,0:T(8,128)S(1)} %get-tuple-element.6, f32[640,256]{1,0:T(8,128)S(1)} %collective-permute-done.24, pred[]{:T(512)S(6)} %eq.7, f32[1280,256]{1,0:T(8,128)} %param.9), kind=kLoop, calls=%fused_computation.24 | loop fusion | flops 3276800 | bytes 7208961 | tf_op jit(solution)/shard_map/convert_element_type | solution.py:107
  182.9 0.0 all-gather.8.cloned.1.call-start
  182.9 1.2 reshape.101
  184.2 28.6 %all_to_all.11 = bf16[64,20,256]{2,1,0:T(8,128)(2,1)S(1)} all-to-all(bf16[64,20,256]{2,1,0:T(8,128)(2,1)S(1)} %reshape.101), channel_id=1, replica_groups=mesh['xh'=2,'core'=2,'y'=4,'xl'=2,'z'=8] {'y','xl','z'}, dimensions={0} | all-to-all | bytes 1310720 | tf_op jit(solution)/shard_map/all_to_all | solution.py:109
  212.8 0.1 copy.36
  213.0 1.3 all_gather_reshape.3
  214.3 10.4 %all-gather.6.cloned.1.call-done = bf16[5120,256]{1,0:T(8,128)(2,1)} async-done(((bf16[1280,256]{1,0:T(8,128)(2,1)}), bf16[5120,256]{1,0:T(8,128)(2,1)}) %all-gather.6.cloned.1.call-update) | async-done | bytes 2621456 | tf_op jit(solution)/shard_map/all_gather | solution.py:108
  224.7 36.1 %all-gather.8.cloned.1.call-done = bf16[4,20,16384]{2,1,0:T(8,128)(2,1)} async-done(((bf16[1,20,16384]{2,1,0:T(8,128)(2,1)}), bf16[4,20,16384]{2,1,0:T(8,128)(2,1)}) %all-gather.8.cloned.1.call-update) | async-done | bytes 2621456 | tf_op jit(solution)/shard_map/all_gather | solution.py:111
  260.8 5.4 %copy.37 = bf16[4,20,16384]{2,0,1:T(4,128)(2,1)} copy(bf16[4,20,16384]{2,1,0:T(8,128)(2,1)} %all-gather.8.cloned.1.call-done) | data formatting | bytes 5242880
  266.2 1.5 copy.49
  (73 shorter events, 0.6 us)
Async XLA Ops:
  7.2 137.2 %all-gather.4.cloned.1.call-start = ((), (), s32[]{:S(2)}) async-start(), calls=%async_computation.2 | async-start | bytes 9437184 | tf_op jit(solution)/shard_map/all_gather | solution.py:89
  8.8 1.5 copy-start.20
  8.8 3.4 %copy-start.19 = (bf16[32,5120]{1,0:T(8,128)(2,1)S(1)}, bf16[32,5120]{1,0:T(8,128)(2,1)}, u32[]{:S(2)}) copy-start(bf16[32,5120]{1,0:T(8,128)(2,1)} %param.6) | copy-start | bytes 983044
  10.2 214.5 %all-gather.6.cloned.1.call-start = ((), (), s32[]{:S(2)}) async-start(), calls=%async_computation.3 | async-start | bytes 3276800 | tf_op jit(solution)/shard_map/all_gather | solution.py:108
  25.4 9.1 %collective-permute-start = (bf16[8,32,384]{2,1,0:T(8,128)(2,1)S(1)}, bf16[8,32,384]{2,1,0:T(8,128)(2,1)S(1)}, u32[]{:S(2)}, u32[]{:S(2)}) collective-permute-start(bf16[8,32,384]{2,1,0:T(8,128)(2,1)S(1)} %slice.40), channel_id=1, source_target_pairs={{0,7},{1,0},{2,1},{3,2},{4,3},{5,4},{6,5},{7,6},{8,15},{9,8},{10,9... | collective-permute-start | bytes 589832 | tf_op jit(solution)/shard_map/ppermute | solution.py:16
  31.1 7.0 %collective-permute-start.3 = (bf16[8,32,384]{2,1,0:T(8,128)(2,1)S(1)}, bf16[8,32,384]{2,1,0:T(8,128)(2,1)S(1)}, u32[]{:S(2)}, u32[]{:S(2)}) collective-permute-start(bf16[8,32,384]{2,1,0:T(8,128)(2,1)S(1)} %slice.40), channel_id=1, source_target_pairs={{0,1},{1,2},{2,3},{3,4},{4,5},{5,6},{6,7},{7,0},{8,9},{9,10},{10,1... | collective-permute-start | bytes 589832 | tf_op jit(solution)/shard_map/ppermute | solution.py:16
  31.1 27.4 %collective-permute-start.13 = (bf16[8,32,256]{2,1,0:T(8,128)(2,1)S(1)}, bf16[8,32,256]{2,1,0:T(8,128)(2,1)S(1)}, u32[]{:S(2)}, u32[]{:S(2)}) collective-permute-start(bf16[8,32,256]{2,1,0:T(8,128)(2,1)S(1)} %slice.45), channel_id=1, source_target_pairs={{0,16},{16,32},{32,48},{48,0},{1,17},{17,33},{33,49},{49,1},{2,18}... | collective-permute-start | bytes 393224 | tf_op jit(solution)/shard_map/ppermute | solution.py:16
  32.4 26.2 %collective-permute-start.12 = (bf16[8,32,256]{2,1,0:T(8,128)(2,1)S(1)}, bf16[8,32,256]{2,1,0:T(8,128)(2,1)S(1)}, u32[]{:S(2)}, u32[]{:S(2)}) collective-permute-start(bf16[8,32,256]{2,1,0:T(8,128)(2,1)S(1)} %slice.45), channel_id=1, source_target_pairs={{0,48},{16,0},{32,16},{48,32},{1,49},{17,1},{33,17},{49,33},{2,50}... | collective-permute-start | bytes 393224 | tf_op jit(solution)/shard_map/ppermute | solution.py:16
  34.6 6.1 %collective-permute-start.1 = (bf16[8,32,384]{2,1,0:T(8,128)(2,1)S(1)}, bf16[8,32,384]{2,1,0:T(8,128)(2,1)S(1)}, u32[]{:S(2)}, u32[]{:S(2)}) collective-permute-start(bf16[8,32,384]{2,1,0:T(8,128)(2,1)S(1)} %collective-permute-done), channel_id=1, source_target_pairs={{0,7},{1,0},{2,1},{3,2},{4,3},{5,4},{6,5},{7,6},{8,15},{9,8},{10,9... | collective-permute-start | bytes 589832 | tf_op jit(solution)/shard_map/ppermute | solution.py:16
  38.1 6.1 %collective-permute-start.4 = (bf16[8,32,384]{2,1,0:T(8,128)(2,1)S(1)}, bf16[8,32,384]{2,1,0:T(8,128)(2,1)S(1)}, u32[]{:S(2)}, u32[]{:S(2)}) collective-permute-start(bf16[8,32,384]{2,1,0:T(8,128)(2,1)S(1)} %collective-permute-done.3), channel_id=1, source_target_pairs={{0,1},{1,2},{2,3},{3,4},{4,5},{5,6},{6,7},{7,0},{8,9},{9,10},{10,1... | collective-permute-start | bytes 589832 | tf_op jit(solution)/shard_map/ppermute | solution.py:16
  40.7 9.3 %collective-permute-start.2 = (bf16[8,32,384]{2,1,0:T(8,128)(2,1)S(1)}, bf16[8,32,384]{2,1,0:T(8,128)(2,1)S(1)}, u32[]{:S(2)}, u32[]{:S(2)}) collective-permute-start(bf16[8,32,384]{2,1,0:T(8,128)(2,1)S(1)} %collective-permute-done.1), channel_id=1, source_target_pairs={{0,7},{1,0},{2,1},{3,2},{4,3},{5,4},{6,5},{7,6},{8,15},{9,8},{10,9... | collective-permute-start | bytes 589832 | tf_op jit(solution)/shard_map/ppermute | solution.py:16
  44.2 5.7 %collective-permute-start.5 = (bf16[8,32,384]{2,1,0:T(8,128)(2,1)S(1)}, bf16[8,32,384]{2,1,0:T(8,128)(2,1)S(1)}, u32[]{:S(2)}, u32[]{:S(2)}) collective-permute-start(bf16[8,32,384]{2,1,0:T(8,128)(2,1)S(1)} %collective-permute-done.4), channel_id=1, source_target_pairs={{0,1},{1,2},{2,3},{3,4},{4,5},{5,6},{6,7},{7,0},{8,9},{9,10},{10,1... | collective-permute-start | bytes 589832 | tf_op jit(solution)/shard_map/ppermute | solution.py:16
  49.9 5.2 %collective-permute-start.6 = (bf16[8,16,384]{2,1,0:T(8,128)(2,1)S(1)}, bf16[8,16,384]{2,1,0:T(8,128)(2,1)S(1)}, u32[]{:S(2)}, u32[]{:S(2)}) collective-permute-start(bf16[8,16,384]{2,1,0:T(8,128)(2,1)S(1)} %slice.41), channel_id=1, source_target_pairs={{0,1},{1,2},{2,3},{3,4},{4,5},{5,6},{6,7},{7,0},{8,9},{9,10},{10,1... | collective-permute-start | bytes 294920 | tf_op jit(solution)/shard_map/ppermute | solution.py:16
  50.0 5.0 %collective-permute-start.7 = (bf16[8,16,384]{2,1,0:T(8,128)(2,1)S(1)}, bf16[8,16,384]{2,1,0:T(8,128)(2,1)S(1)}, u32[]{:S(2)}, u32[]{:S(2)}) collective-permute-start(bf16[8,16,384]{2,1,0:T(8,128)(2,1)S(1)} %slice.42), channel_id=1, source_target_pairs={{0,7},{1,0},{2,1},{3,2},{4,3},{5,4},{6,5},{7,6},{8,15},{9,8},{10,9... | collective-permute-start | bytes 294920 | tf_op jit(solution)/shard_map/ppermute | solution.py:16
  55.2 58.7 %copy-start.8 = (bf16[8,8,32,384]{3,2,1,0:T(8,128)(2,1)}, bf16[8,8,32,384]{3,2,1,0:T(8,128)(2,1)S(1)}, u32[]{:S(2)}) copy-start(bf16[8,8,32,384]{3,2,1,0:T(8,128)(2,1)S(1)} %bitcast_dynamic-update-slice_fusion.6) | copy-start | bytes 4718596
  55.2 58.5 %collective-permute-start.9 = (bf16[8,8,32,384]{3,2,1,0:T(8,128)(2,1)S(1)}, bf16[8,8,32,384]{3,2,1,0:T(8,128)(2,1)S(1)}, u32[]{:S(2)}, u32[]{:S(2)}) collective-permute-start(bf16[8,8,32,384]{3,2,1,0:T(8,128)(2,1)S(1)} %bitcast_dynamic-update-slice_fusion.6), channel_id=1, source_target_pairs={{0,16},{16,32},{32,48},{48,0},{1,17},{17,33},{33,49},{49,1},{2,18}... | collective-permute-start | bytes 4718600 | tf_op jit(solution)/shard_map/ppermute | solution.py:16
  56.6 58.8 %collective-permute-start.8 = (bf16[8,8,32,384]{3,2,1,0:T(8,128)(2,1)S(1)}, bf16[8,8,32,384]{3,2,1,0:T(8,128)(2,1)S(1)}, u32[]{:S(2)}, u32[]{:S(2)}) collective-permute-start(bf16[8,8,32,384]{3,2,1,0:T(8,128)(2,1)S(1)} %bitcast_dynamic-update-slice_fusion.6), channel_id=1, source_target_pairs={{0,48},{16,0},{32,16},{48,32},{1,49},{17,1},{33,17},{49,33},{2,50}... | collective-permute-start | bytes 4718600 | tf_op jit(solution)/shard_map/ppermute | solution.py:16
  58.5 31.6 %collective-permute-start.14 = (bf16[8,16,256]{2,1,0:T(8,128)(2,1)S(1)}, bf16[8,16,256]{2,1,0:T(8,128)(2,1)S(1)}, u32[]{:S(2)}, u32[]{:S(2)}) collective-permute-start(bf16[8,16,256]{2,1,0:T(8,128)(2,1)S(1)} %slice.46), channel_id=1, source_target_pairs={{0,16},{16,32},{32,48},{48,0},{1,17},{17,33},{33,49},{49,1},{2,18}... | collective-permute-start | bytes 196616 | tf_op jit(solution)/shard_map/ppermute | solution.py:16
  58.7 31.4 %collective-permute-start.15 = (bf16[8,16,256]{2,1,0:T(8,128)(2,1)S(1)}, bf16[8,16,256]{2,1,0:T(8,128)(2,1)S(1)}, u32[]{:S(2)}, u32[]{:S(2)}) collective-permute-start(bf16[8,16,256]{2,1,0:T(8,128)(2,1)S(1)} %slice.47), channel_id=1, source_target_pairs={{0,48},{16,0},{32,16},{48,32},{1,49},{17,1},{33,17},{49,33},{2,50}... | collective-permute-start | bytes 196616 | tf_op jit(solution)/shard_map/ppermute | solution.py:16
  90.2 9.3 %collective-permute-start.19 = (bf16[4,4,2,32,256]{4,3,2,1,0:T(8,128)(2,1)S(1)}, bf16[4,4,2,32,256]{4,3,2,1,0:T(8,128)(2,1)S(1)}, u32[]{:S(2)}, u32[]{:S(2)}) collective-permute-start(bf16[4,4,2,32,256]{4,3,2,1,0:T(8,128)(2,1)S(1)} %pad_maximum_fusion.1), channel_id=1, source_target_pairs={{0,1},{1,2},{2,3},{3,4},{4,5},{5,6},{6,7},{7,0},{8,9},{9,10},{10,1... | collective-permute-start | bytes 1572872 | tf_op jit(solution)/shard_map/ppermute | solution.py:16
  90.3 10.0 %collective-permute-start.16 = (bf16[4,4,2,32,256]{4,3,2,1,0:T(8,128)(2,1)S(1)}, bf16[4,4,2,32,256]{4,3,2,1,0:T(8,128)(2,1)S(1)}, u32[]{:S(2)}, u32[]{:S(2)}) collective-permute-start(bf16[4,4,2,32,256]{4,3,2,1,0:T(8,128)(2,1)S(1)} %pad_maximum_fusion.1), channel_id=1, source_target_pairs={{0,7},{1,0},{2,1},{3,2},{4,3},{5,4},{6,5},{7,6},{8,15},{9,8},{10,9... | collective-permute-start | bytes 1572872 | tf_op jit(solution)/shard_map/ppermute | solution.py:16
  99.5 11.4 %collective-permute-start.20 = (bf16[4,4,2,32,256]{4,3,2,1,0:T(8,128)(2,1)S(1)}, bf16[4,4,2,32,256]{4,3,2,1,0:T(8,128)(2,1)S(1)}, u32[]{:S(2)}, u32[]{:S(2)}) collective-permute-start(bf16[4,4,2,32,256]{4,3,2,1,0:T(8,128)(2,1)S(1)} %collective-permute-done.19), channel_id=1, source_target_pairs={{0,1},{1,2},{2,3},{3,4},{4,5},{5,6},{6,7},{7,0},{8,9},{9,10},{10,1... | collective-permute-start | bytes 1572872 | tf_op jit(solution)/shard_map/ppermute | solution.py:16
  99.5 0.8 copy-start.10
  100.3 10.6 %collective-permute-start.17 = (bf16[4,4,2,32,256]{4,3,2,1,0:T(8,128)(2,1)S(1)}, bf16[4,4,2,32,256]{4,3,2,1,0:T(8,128)(2,1)S(1)}, u32[]{:S(2)}, u32[]{:S(2)}) collective-permute-start(bf16[4,4,2,32,256]{4,3,2,1,0:T(8,128)(2,1)S(1)} %collective-permute-done.16), channel_id=1, source_target_pairs={{0,7},{1,0},{2,1},{3,2},{4,3},{5,4},{6,5},{7,6},{8,15},{9,8},{10,9... | collective-permute-start | bytes 1572872 | tf_op jit(solution)/shard_map/ppermute | solution.py:16
  103.0 0.8 copy-start.12
  110.9 4.5 %copy-start.14 = (bf16[4,4,2,32,256]{4,3,2,1,0:T(8,128)(2,1)}, bf16[4,4,2,32,256]{4,3,2,1,0:T(8,128)(2,1)S(1)}, u32[]{:S(2)}) copy-start(bf16[4,4,2,32,256]{4,3,2,1,0:T(8,128)(2,1)S(1)} %collective-permute-done.20) | copy-start | bytes 1572868
  110.9 12.5 %collective-permute-start.21 = (bf16[4,4,2,32,256]{4,3,2,1,0:T(8,128)(2,1)S(1)}, bf16[4,4,2,32,256]{4,3,2,1,0:T(8,128)(2,1)S(1)}, u32[]{:S(2)}, u32[]{:S(2)}) collective-permute-start(bf16[4,4,2,32,256]{4,3,2,1,0:T(8,128)(2,1)S(1)} %collective-permute-done.20), channel_id=1, source_target_pairs={{0,1},{1,2},{2,3},{3,4},{4,5},{5,6},{6,7},{7,0},{8,9},{9,10},{10,1... | collective-permute-start | bytes 1572872 | tf_op jit(solution)/shard_map/ppermute | solution.py:16
  110.9 4.5 %copy-start.16 = (bf16[4,4,2,32,256]{4,3,2,1,0:T(8,128)(2,1)}, bf16[4,4,2,32,256]{4,3,2,1,0:T(8,128)(2,1)S(1)}, u32[]{:S(2)}) copy-start(bf16[4,4,2,32,256]{4,3,2,1,0:T(8,128)(2,1)S(1)} %collective-permute-done.17) | copy-start | bytes 1572868
  110.9 12.7 %collective-permute-start.18 = (bf16[4,4,2,32,256]{4,3,2,1,0:T(8,128)(2,1)S(1)}, bf16[4,4,2,32,256]{4,3,2,1,0:T(8,128)(2,1)S(1)}, u32[]{:S(2)}, u32[]{:S(2)}) collective-permute-start(bf16[4,4,2,32,256]{4,3,2,1,0:T(8,128)(2,1)S(1)} %collective-permute-done.17), channel_id=1, source_target_pairs={{0,7},{1,0},{2,1},{3,2},{4,3},{5,4},{6,5},{7,6},{8,15},{9,8},{10,9... | collective-permute-start | bytes 1572872 | tf_op jit(solution)/shard_map/ppermute | solution.py:16
  113.8 1.7 copy-start
  113.9 19.4 %collective-permute-start.10 = (bf16[4,8,32,384]{3,2,1,0:T(8,128)(2,1)S(1)}, bf16[4,8,32,384]{3,2,1,0:T(8,128)(2,1)S(1)}, u32[]{:S(2)}, u32[]{:S(2)}) collective-permute-start(bf16[4,8,32,384]{3,2,1,0:T(8,128)(2,1)S(1)} %slice.43), channel_id=1, source_target_pairs={{0,16},{16,32},{32,48},{48,0},{1,17},{17,33},{33,49},{49,1},{2,18}... | collective-permute-start | bytes 2359304 | tf_op jit(solution)/shard_map/ppermute | solution.py:16
  115.4 17.9 %copy-start.2 = (bf16[8,8,32,384]{3,2,1,0:T(8,128)(2,1)}, bf16[8,8,32,384]{3,2,1,0:T(8,128)(2,1)S(1)}, u32[]{:S(2)}) copy-start(bf16[8,8,32,384]{3,2,1,0:T(8,128)(2,1)S(1)} %collective-permute-done.8) | copy-start | bytes 4718596
  115.5 17.8 %collective-permute-start.11 = (bf16[4,8,32,384]{3,2,1,0:T(8,128)(2,1)S(1)}, bf16[4,8,32,384]{3,2,1,0:T(8,128)(2,1)S(1)}, u32[]{:S(2)}, u32[]{:S(2)}) collective-permute-start(bf16[4,8,32,384]{3,2,1,0:T(8,128)(2,1)S(1)} %slice.44), channel_id=1, source_target_pairs={{0,48},{16,0},{32,16},{48,32},{1,49},{17,1},{33,17},{49,33},{2,50}... | collective-permute-start | bytes 2359304 | tf_op jit(solution)/shard_map/ppermute | solution.py:16
  123.5 10.1 %copy-start.4 = (bf16[4,4,2,32,256]{4,3,2,1,0:T(8,128)(2,1)}, bf16[4,4,2,32,256]{4,3,2,1,0:T(8,128)(2,1)S(1)}, u32[]{:S(2)}) copy-start(bf16[4,4,2,32,256]{4,3,2,1,0:T(8,128)(2,1)S(1)} %collective-permute-done.21) | copy-start | bytes 1572868
  123.5 9.7 %collective-permute-start.22 = (bf16[2,4,2,32,256]{4,3,2,1,0:T(8,128)(2,1)S(1)}, bf16[2,4,2,32,256]{4,3,2,1,0:T(8,128)(2,1)S(1)}, u32[]{:S(2)}, u32[]{:S(2)}) collective-permute-start(bf16[2,4,2,32,256]{4,3,2,1,0:T(8,128)(2,1)S(1)} %slice.48), channel_id=1, source_target_pairs={{0,1},{1,2},{2,3},{3,4},{4,5},{5,6},{6,7},{7,0},{8,9},{9,10},{10,1... | collective-permute-start | bytes 786440 | tf_op jit(solution)/shard_map/ppermute | solution.py:16
  123.7 9.6 %copy-start.6 = (bf16[4,4,2,32,256]{4,3,2,1,0:T(8,128)(2,1)}, bf16[4,4,2,32,256]{4,3,2,1,0:T(8,128)(2,1)S(1)}, u32[]{:S(2)}) copy-start(bf16[4,4,2,32,256]{4,3,2,1,0:T(8,128)(2,1)S(1)} %collective-permute-done.18) | copy-start | bytes 1572868
  123.7 9.5 %collective-permute-start.23 = (bf16[2,4,2,32,256]{4,3,2,1,0:T(8,128)(2,1)S(1)}, bf16[2,4,2,32,256]{4,3,2,1,0:T(8,128)(2,1)S(1)}, u32[]{:S(2)}, u32[]{:S(2)}) collective-permute-start(bf16[2,4,2,32,256]{4,3,2,1,0:T(8,128)(2,1)S(1)} %slice.49), channel_id=1, source_target_pairs={{0,7},{1,0},{2,1},{3,2},{4,3},{5,4},{6,5},{7,6},{8,15},{9,8},{10,9... | collective-permute-start | bytes 786440 | tf_op jit(solution)/shard_map/ppermute | solution.py:16
  144.4 1.4 copy-start.1
  145.8 1.4 copy-start.3
  147.2 1.0 copy-start.5
  148.2 1.0 copy-start.7
  149.3 1.4 copy-start.9
  150.7 1.0 copy-start.11
  151.7 1.0 copy-start.13
  152.8 1.0 copy-start.15
  153.8 1.0 copy-start.17
  164.7 14.4 %collective-permute-start.24 = (f32[640,256]{1,0:T(8,128)}, f32[640,256]{1,0:T(8,128)S(1)}, u32[]{:S(2)}, u32[]{:S(2)}) collective-permute-start(f32[640,256]{1,0:T(8,128)} %get-tuple-element.7), channel_id=1, source_target_pairs={{0,8},{8,0},{1,9},{9,1},{2,10},{10,2},{3,11},{11,3},{4,12},{12,4},... | collective-permute-start | bytes 1966088 | tf_op jit(solution)/shard_map/ppermute | solution.py:16
  182.9 77.9 %all-gather.8.cloned.1.call-start = ((), (), s32[]{:S(2)}) async-start(), calls=%async_computation.4 | async-start | bytes 3932160 | tf_op jit(solution)/shard_map/all_gather | solution.py:111
  224.7 41.5 %copy-start.18 = (bf16[5120,256]{1,0:T(8,128)(2,1)S(1)}, bf16[5120,256]{1,0:T(8,128)(2,1)}, u32[]{:S(2)}) copy-start(bf16[5120,256]{1,0:T(8,128)(2,1)} %all-gather.6.cloned.1.call-done) | copy-start | bytes 7864324
Sparse Core Ops, SparseCore 0:
  10.4 133.9 all-gather.3
  183.0 41.6 all-gather.5
  227.1 33.6 all-gather.7

commit v2 on v0

v2 whole, which is shorter than its diff:
```python
import functools

import jax
import jax.numpy as jnp
from jax import lax
from jax.experimental import pallas as pl
from jax.experimental.pallas import tpu as pltpu
from jax.sharding import Mesh, PartitionSpec as P

REGION = ("xh", "core")
SHARD = ("y", "xl", "z")
WIDE = 384
NARROW = 256


def shift(x, axis, n, by):
    return lax.ppermute(x, axis, [(i, (i + by) % n) for i in range(n)])


def both(pair, axis, n):
    return shift(pair[0], axis, n, 1), shift(pair[1], axis, n, -1)


def halves(pair, axis, n, dim):
    size = pair[0].shape[dim] // 2
    return both(
        (lax.slice_in_dim(pair[0], 0, size, axis=dim), lax.slice_in_dim(pair[1], size, 2 * size, axis=dim)),
        axis, n)


def after(values, others):
    return lax.optimization_barrier((values, others))[0]


def gradient_kernel(js, ms, first, last, *refs):
    role, refs = refs[0], refs[1:]
    wide, refs = refs[: len(js)], refs[len(js) :]
    narrow, refs = refs[: len(ms)], refs[len(ms) :]
    cots, refs = refs[0], refs[1:]
    before, refs = ((), refs) if first else (refs[:2], refs[2:])
    old, refs = (refs[:2], refs[2:]) if last else ((), refs)
    low = lax.axis_index("xl")
    ys = [lax.rem(lax.axis_index("y") + j, 4) for j in range(4)]
    zs = [lax.rem(lax.axis_index("z") + m, 8) for m in range(8)]
    shares = [jnp.where(role[r] < 2, 0.25, jnp.where(role[r] == 2, 0.5, 0.0)) for r in range(4)]
    for side in range(2):
        column = low if side == 0 else 1 - low
        sources = [(cots.at[region // 2, column, region % 2], region) for region in range(4)]
        total = None if first else before[side][:WIDE, :]
        for cot, region in sources:
            for ref, j in zip(wide, js):
                rows = jnp.concatenate([cot[ys[j], l, zs[m]] for l in range(2) for m in range(8)], 0)
                part = shares[region] * lax.dot_general(
                    ref[region], rows, (((0,), (0,)), ((), ())), preferred_element_type=jnp.float32)
                total = part if total is None else total + part
        refs[side][:WIDE, :] = total
        total = None if first else before[side][WIDE:, :]
        for cot, region in sources:
            for ref, m in zip(narrow, ms):
                rows = jnp.concatenate([cot[ys[j], l, zs[m]] for j in range(4) for l in range(2)], 0)
                part = shares[region] * lax.dot_general(
                    ref[region], rows, (((0,), (0,)), ((), ())), preferred_element_type=jnp.float32)
                total = part if total is None else total + part
        refs[side][WIDE:, :] = total
        if last:
            for target in range(32):
                at = slice(20 * target, 20 * target + 20)
                new = step(refs[side][at, :], old[side][0, at, :], old[side][1, at, :])[0]
                refs[2][target, column] = new.astype(jnp.bfloat16)


def gradient(role, wide, narrow, cots, before=(), old=()):
    js, ms = tuple(wide), tuple(narrow)
    tile = jax.ShapeDtypeStruct((640, 256), jnp.float32)
    rows = jax.ShapeDtypeStruct((32, 2, 20, 256), jnp.bfloat16)
    operands = (role, *wide.values(), *narrow.values(), cots, *before, *old)
    at = len(operands) - len(before) - len(old)
    share = (len(js) / 4 * WIDE + len(ms) / 8 * NARROW) / 640
    return pl.pallas_call(
        functools.partial(gradient_kernel, js, ms, not before, bool(old)),
        out_shape=(tile, tile, rows) if old else (tile, tile),
        in_specs=[pl.BlockSpec(memory_space=pltpu.SMEM)]
        + [pl.BlockSpec(memory_space=pltpu.VMEM)] * (len(operands) - 1),
        out_specs=[pl.BlockSpec(memory_space=pltpu.VMEM)] * (3 if old else 2),
        input_output_aliases={at: 0, at + 1: 1} if before else {},
        compiler_params=pltpu.CompilerParams(vmem_limit_bytes=8 << 20),
        cost_estimate=pl.CostEstimate(
            flops=int(share * 2 * 8192 * 640 * 512), bytes_accessed=int(share * (18 << 20)), transcendentals=0),
        name="gradient",
    )(*operands)


def step(delta, master, momentum):
    new_momentum = 0.9 * momentum + delta
    return master - 0.7 * (delta + 0.9 * new_momentum), new_momentum


def in_order(low, own, other, axis):
    return jnp.where(low == 0, jnp.stack([own, other], axis), jnp.stack([other, own], axis))


def per_device(region_role, tokens, cotangent, master, momentum):
    low, core = lax.axis_index("xl"), lax.axis_index("core")

    blocks = tokens.reshape(32, 4, 4, 2, 160).transpose(1, 3, 0, 2, 4).reshape(8, 32, 640)
    here = lax.all_to_all(blocks, ("xh", "core", "xl"), split_axis=0, concat_axis=0, tiled=True)
    a0, b0 = here[:, :, :WIDE], here[:, :, WIDE:]

    cots = lax.all_gather(cotangent, ("xh", "xl", "core"), axis=0, tiled=True).reshape(2, 2, 2, 4, 2, 8, 32, 256)

    a1, b1 = both((a0, a0), "z", 8), both((b0, b0), "y", 4)
    a1, b1 = lax.optimization_barrier((a1, b1))
    a2, b2 = both(a1, "z", 8), halves(b1, "y", 4, 1)
    a2, b2 = lax.optimization_barrier((a2, b2))
    a3 = both(a2, "z", 8)
    narrow = [b0, b1[1], jnp.concatenate(b2, 1), b1[0]]
    narrow = jnp.concatenate([t.reshape(4, 1, 2, 32, NARROW) for t in narrow], 1)
    a3, narrow = lax.optimization_barrier((a3, narrow))
    a4 = halves(a3, "z", 8, 1)
    n1 = both((narrow, narrow), "z", 8)
    wide = [a0, a1[1], a2[1], a3[1], jnp.concatenate(a4, 1), a3[0], a2[0], a1[0]]
    wide = jnp.concatenate([t[:, None] for t in wide], 1)
    w1 = both((wide, wide), "y", 4)

    old = jnp.stack([master, momentum]).reshape(2, 4, 2, 160, 256)
    mine = lax.dynamic_index_in_dim(old, low, 2, keepdims=False)
    theirs = shift(after(lax.dynamic_index_in_dim(old, 1 - low, 2, keepdims=False), narrow), "xl", 2, 1)
    mine, theirs = mine.reshape(2, 640, 256), theirs.reshape(2, 640, 256)

    n2 = both(n1, "z", 8)
    w1, theirs = lax.optimization_barrier((w1, theirs))
    w2 = halves(w1, "y", 4, 0)
    n3 = both(n2, "z", 8)
    shaped = lambda t: t.reshape(4, -1, t.shape[-1])
    tile = gradient(
        region_role,
        {0: shaped(wide), 1: shaped(w1[1]), 3: shaped(w1[0])},
        {0: shaped(narrow), 1: shaped(n1[1]), 7: shaped(n1[0]), 2: shaped(n2[1]), 6: shaped(n2[0])}, cots)
    n3, tile = lax.optimization_barrier((n3, tile))
    n4 = halves(n3, "z", 8, 0)
    own, other, rows = gradient(
        region_role,
        {2: shaped(jnp.concatenate(w2, 0))},
        {3: shaped(n3[1]), 5: shaped(n3[0]), 4: shaped(jnp.concatenate(n4, 0))}, cots, tile, (mine, theirs))

    came = shift(other, "xl", 2, 1)
    rows = lax.all_to_all(rows, ("y", "z"), split_axis=0, concat_axis=0, tiled=True)
    rows = rows.reshape(4, 8, 2, 20, 256).transpose(3, 0, 2, 1, 4).reshape(20, 16384)
    far = shift(rows, "xh", 2, 1)
    near = shift(rows, "core", 2, 1)
    far_near = shift(far, "core", 2, 1)
    rollout_weight = in_order(
        lax.axis_index("xh"), in_order(core, rows, near, 0), in_order(core, far, far_near, 0), 0)
    rollout_weight = rollout_weight.reshape(4, 20, 16384)

    delta = in_order(low, own.reshape(4, 160, 256), came.reshape(4, 160, 256), 1).reshape(1280, 256)
    new_master, new_momentum = step(delta, master, momentum)
    fresh = new_master.astype(jnp.bfloat16)
    learner_weight = lax.all_gather(fresh, REGION, axis=0, tiled=True)
    return new_master, new_momentum, learner_weight, rollout_weight


def solution(mesh):
    fine = Mesh(mesh.devices.reshape(2, 2, 4, 2, 8), REGION + SHARD)
    tile = P(REGION, SHARD)
    return jax.shard_map(
        per_device,
        mesh=fine,
        in_specs=(P(), P(REGION + SHARD, None), tile, tile, tile),
        out_specs=(tile, tile, P(None, SHARD), P(None, SHARD, None)),
        check_vma=False,
    )
```

time: 555 us -> 204 us (0.37)
  waiting for transfers between devices: 434 us -> 67.3 us
  blocking collectives: 71.9 us -> 13.1 us
  starting transfers between devices: 0.12 us -> 58.4 us
  local copies, waits for them, and re-layouts: 16.7 us -> 31.5 us
  matrix products: 12.7 us -> 0 us
  Pallas kernels: 0 us -> 9.97 us
    all_gather x2, waiting for transfers between devices: 336 us -> 2.1 us  [the longest x1 2.09 us: per_device(): learner_weight = lax.all_gather(fresh, REGION, axis=0, tiled=True)]
    reduce_scatter x1 -> x0, waiting for transfers between devices: 96.6 us -> none  [per_device(): lax.psum_scatter(share * grad, 'region', scatter_dimension=0, tiled=True)]
    ppermute x0 -> x29, waiting for transfers between devices: none -> 61 us  [shift(): return lax.ppermute(x, axis, [(i, (i + by) % n) for i in range(n)])]
    all_to_all x1, blocking collectives: 71.9 us -> 13.1 us  [per_device(): lax.all_to_all(blocks, ('xh', 'core', 'xl'), split_axis=0, concat_axis=0,...]
    ppermute x0 -> x29, starting transfers between devices: none -> 50.2 us  [shift(): return lax.ppermute(x, axis, [(i, (i + by) % n) for i in range(n)])]
    unnamed x7 -> x40, local copies, waits for them, and re-layouts: 1.51 us -> 21.7 us
    dot_general x1 -> x0, matrix products: 12.7 us -> none  [per_device(): lax.dot_general(lax.all_gather(tokens, 'shard', axis=0, tiled=True), cota...]
    pallas_call x0 -> x2, Pallas kernels: none -> 9.97 us  [gradient(): pl.pallas_call(functools.partial(gradient_kernel, js, ms, not before, boo...]
  transfers between devices with their start and end apart: 3 -> 32, of which waited for: 3 -> 14; matrix products, arithmetic and copies ran while one was open for 0% -> 12% of each run, Pallas kernels for 0% -> 3%
where the time goes in v2:
time: 204 us
  waiting for transfers between devices  67.3 us (33%)
  starting transfers between devices  58.4 us (29%)
  local copies, waits for them, and re-layouts  31.5 us (15%)
  between operations  14.4 us (7%)
  blocking collectives  13.1 us (6%)
  Pallas kernels  9.97 us (5%)
  other arithmetic  9.21 us (5%)
    ppermute x29, waiting for transfers between devices, shift(): return lax.ppermute(x, axis, [(i, (i + by) % n) for i in range(n)])  61 us
    ppermute x29, starting transfers between devices, shift(): return lax.ppermute(x, axis, [(i, (i + by) % n) for i in range(n)])  50.2 us
    unnamed x40, local copies, waits for them, and re-layouts  21.7 us
    all_to_all x1, blocking collectives, per_device(): lax.all_to_all(blocks, ('xh', 'core', 'xl'), split_axis=0, concat_axis=0,...  13.1 us
    pallas_call x2, Pallas kernels, gradient(): pl.pallas_call(functools.partial(gradient_kernel, js, ms, not before, boo...  9.97 us
    all_to_all x1, starting transfers between devices, per_device(): lax.all_to_all(rows, ('y', 'z'), split_axis=0, concat_axis=0, tiled=True)  8.09 us
  transfers between devices with their start and end apart: 32, of which 14 were waited for; matrix products, arithmetic and copies ran while one was open for 12% of the time, Pallas kernels for 3%

profile of v2, /device:TPU:1, one launch (start us, length us, event | category | flops | bytes accessed | tf_op | source)
XLA Modules:
  0.0 203.8 jit_solution(2751827483044339152)
XLA Ops:
  7.9 1.6 reshape.211
  10.0 13.1 %all_to_all.10 = bf16[8,32,640]{2,1,0:T(8,128)(2,1)S(1)} all-to-all(bf16[8,32,640]{2,1,0:T(8,128)(2,1)S(1)} %reshape.212), channel_id=1, replica_groups=mesh['xh'=2,'core'=2,'y'=4,'xl'=2,'z'=8] {'xh','core','xl'}, dimensions={0} | all-to-all | bytes 655360 | tf_op jit(solution)/shard_map/all_to_all | solution.py:106
  23.1 1.4 collective-permute-start.2
  24.5 1.5 collective-permute-start.3
  26.0 1.7 collective-permute-start
  27.8 4.0 %collective-permute-start.1 = (bf16[8,32,384]{2,1,0:T(8,128)(2,1)S(1)}, bf16[8,32,384]{2,1,0:T(8,128)(2,1)S(1)}, u32[]{:S(2)}, u32[]{:S(2)}) collective-permute-start(bf16[8,32,384]{2,1,0:T(8,128)(2,1)S(1)} %slice.40), channel_id=1, source_target_pairs={{0,7},{1,0},{2,1},{3,2},{4,3},{5,4},{6,5},{7,6},{8,15},{9,8},{10,9... | collective-permute-start | bytes 589832 | tf_op jit(solution)/shard_map/ppermute | solution.py:17
  32.5 3.4 %collective-permute-done = bf16[8,32,384]{2,1,0:T(8,128)(2,1)S(1)} collective-permute-done((bf16[8,32,384]{2,1,0:T(8,128)(2,1)S(1)}, bf16[8,32,384]{2,1,0:T(8,128)(2,1)S(1)}, u32[]{:S(2)}, u32[]{:S(2)}) %collective-permute-start) | collective-permute-done | bytes 196640 | tf_op jit(solution)/shard_map/ppermute | solution.py:17
  35.9 2.7 %collective-permute-start.5 = (bf16[8,32,384]{2,1,0:T(8,128)(2,1)S(1)}, bf16[8,32,384]{2,1,0:T(8,128)(2,1)S(1)}, u32[]{:S(2)}, u32[]{:S(2)}) collective-permute-start(bf16[8,32,384]{2,1,0:T(8,128)(2,1)S(1)} %collective-permute-done.1), channel_id=1, source_target_pairs={{0,7},{1,0},{2,1},{3,2},{4,3},{5,4},{6,5},{7,6},{8,15},{9,8},{10,9... | collective-permute-start | bytes 589832 | tf_op jit(solution)/shard_map/ppermute | solution.py:17
  38.6 2.7 %collective-permute-start.7 = (bf16[8,16,256]{2,1,0:T(8,128)(2,1)S(1)}, bf16[8,16,256]{2,1,0:T(8,128)(2,1)S(1)}, u32[]{:S(2)}, u32[]{:S(2)}) collective-permute-start(bf16[8,16,256]{2,1,0:T(8,128)(2,1)S(1)} %slice.33), channel_id=1, source_target_pairs={{0,48},{16,0},{32,16},{48,32},{1,49},{17,1},{33,17},{49,33},{2,50}... | collective-permute-start | bytes 196616 | tf_op jit(solution)/shard_map/ppermute | solution.py:17
  41.2 0.7 bitcast_dynamic-update-slice_fusion.4
  41.9 1.3 collective-permute-done.6
  43.6 2.4 %collective-permute-start.9 = (bf16[8,32,384]{2,1,0:T(8,128)(2,1)S(1)}, bf16[8,32,384]{2,1,0:T(8,128)(2,1)S(1)}, u32[]{:S(2)}, u32[]{:S(2)}) collective-permute-start(bf16[8,32,384]{2,1,0:T(8,128)(2,1)S(1)} %collective-permute-done.5), channel_id=1, source_target_pairs={{0,7},{1,0},{2,1},{3,2},{4,3},{5,4},{6,5},{7,6},{8,15},{9,8},{10,9... | collective-permute-start | bytes 589832 | tf_op jit(solution)/shard_map/ppermute | solution.py:17
  46.2 0.7 bitcast_dynamic-update-slice_fusion.3
  46.9 2.6 %collective-permute-done.8 = bf16[8,32,384]{2,1,0:T(8,128)(2,1)S(1)} collective-permute-done((bf16[8,32,384]{2,1,0:T(8,128)(2,1)S(1)}, bf16[8,32,384]{2,1,0:T(8,128)(2,1)S(1)}, u32[]{:S(2)}, u32[]{:S(2)}) %collective-permute-start.8) | collective-permute-done | bytes 196640 | tf_op jit(solution)/shard_map/ppermute | solution.py:17
  50.1 2.3 %collective-permute-start.11 = (bf16[8,16,384]{2,1,0:T(8,128)(2,1)S(1)}, bf16[8,16,384]{2,1,0:T(8,128)(2,1)S(1)}, u32[]{:S(2)}, u32[]{:S(2)}) collective-permute-start(bf16[8,16,384]{2,1,0:T(8,128)(2,1)S(1)} %slice.35), channel_id=1, source_target_pairs={{0,7},{1,0},{2,1},{3,2},{4,3},{5,4},{6,5},{7,6},{8,15},{9,8},{10,9... | collective-permute-start | bytes 294920 | tf_op jit(solution)/shard_map/ppermute | solution.py:17
  52.4 0.7 bitcast_dynamic-update-slice_fusion.2
  53.1 1.6 collective-permute-done.10
  54.7 0.7 fusion.5
  55.4 0.7 bitcast_dynamic-update-slice_fusion.1
  56.1 0.7 bitcast_dynamic-update-slice_fusion
  56.8 0.7 bitcast_dynamic-update-slice_fusion.6
  57.5 2.7 %collective-permute-start.13 = (bf16[8,8,32,384]{3,2,1,0:T(8,128)(2,1)}, bf16[8,8,32,384]{3,2,1,0:T(8,128)(2,1)}, u32[]{:S(2)}, u32[]{:S(2)}) collective-permute-start(bf16[8,8,32,384]{3,2,1,0:T(8,128)(2,1)} %bitcast_dynamic-update-slice_fusion.6), channel_id=1, source_target_pairs={{0,48},{16,0},{32,16},{48,32},{1,49},{17,1},{33,17},{49,33},{2,50}... | collective-permute-start | bytes 4718600 | tf_op jit(solution)/shard_map/ppermute | solution.py:17
  60.2 1.9 fusion
  62.2 2.0 %collective-permute-start.17 = (bf16[4,4,2,32,256]{4,3,2,1,0:T(8,128)(2,1)S(1)}, bf16[4,4,2,32,256]{4,3,2,1,0:T(8,128)(2,1)S(1)}, u32[]{:S(2)}, u32[]{:S(2)}) collective-permute-start(bf16[4,4,2,32,256]{4,3,2,1,0:T(8,128)(2,1)S(1)} %pad_maximum_fusion.1), channel_id=1, source_target_pairs={{0,1},{1,2},{2,3},{3,4},{4,5},{5,6},{6,7},{7,0},{8,9},{9,10},{10,1... | collective-permute-start | bytes 1572872 | tf_op jit(solution)/shard_map/ppermute | solution.py:17
  64.2 0.9 collective-permute-start.20
  65.1 6.8 %collective-permute-done.17 = bf16[4,4,2,32,256]{4,3,2,1,0:T(8,128)(2,1)S(1)} collective-permute-done((bf16[4,4,2,32,256]{4,3,2,1,0:T(8,128)(2,1)S(1)}, bf16[4,4,2,32,256]{4,3,2,1,0:T(8,128)(2,1)S(1)}, u32[]{:S(2)}, u32[]{:S(2)}) %collective-permute-start.17) | collective-permute-done | bytes 524320 | tf_op jit(solution)/shard_map/ppermute | solution.py:17
  71.9 0.8 collective-permute-start.18
  72.7 0.8 copy-done.8
  73.5 1.9 collective-permute-start.21
  75.4 0.8 copy-done.10
  76.2 11.1 %collective-permute-done.14 = f32[2,4,160,256]{3,2,1,0:T(8,128)S(1)} collective-permute-done((f32[2,4,160,256]{3,2,1,0:T(8,128)S(1)}, f32[2,4,160,256]{3,2,1,0:T(8,128)S(1)}, u32[]{:S(2)}, u32[]{:S(2)}) %collective-permute-start.14) | collective-permute-done | bytes 1310752 | tf_op jit(solution)/shard_map/ppermute | solution.py:17
  87.3 1.1 copy-done.4
  88.3 1.8 collective-permute-done.12
  90.2 1.0 slice.36
  91.7 2.1 %slice.37 = bf16[4,8,32,384]{3,2,1,0:T(8,128)(2,1)} slice(bf16[8,8,32,384]{3,2,1,0:T(8,128)(2,1)} %collective-permute-done.13), slice={[4:8], [0:8], [0:32], [0:384]} | slice | bytes 1572864 | tf_op jit(solution)/shard_map/slice | solution.py:27
  93.8 2.1 %collective-permute-start.16 = (bf16[4,8,32,384]{3,2,1,0:T(8,128)(2,1)}, bf16[4,8,32,384]{3,2,1,0:T(8,128)(2,1)}, u32[]{:S(2)}, u32[]{:S(2)}) collective-permute-start(bf16[4,8,32,384]{3,2,1,0:T(8,128)(2,1)} %slice.37), channel_id=1, source_target_pairs={{0,48},{16,0},{32,16},{48,32},{1,49},{17,1},{33,17},{49,33},{2,50}... | collective-permute-start | bytes 2359304 | tf_op jit(solution)/shard_map/ppermute | solution.py:17
  96.0 1.5 collective-permute-start.19
  97.5 1.3 collective-permute-start.22
  98.8 3.4 %copy-done = bf16[16384,256]{1,0:T(8,128)(2,1)S(1)} copy-done((bf16[16384,256]{1,0:T(8,128)(2,1)S(1)}, bf16[16384,256]{1,0:T(8,128)(2,1)}, u32[]{:S(2)}) %copy-start) | copy-done | bytes 8388632
  102.1 1.0 copy-done.3
  103.2 1.0 copy-done.9
  104.2 1.0 copy-done.11
  105.3 6.4 %gradient.2 = (f32[640,256]{1,0:T(8,128)S(1)}, f32[640,256]{1,0:T(8,128)S(1)}) custom-call(s32[4]{0:T(128)S(1)} %copy-done.12, bf16[4,512,384]{2,1,0:T(8,128)(2,1)} %bitcast.25.refs_1_, bf16[4,512,384]{2,1,0:T(8,128)(2,1)} %bitcast.26.refs_2_, bf16[4,512,384]{2,1,0:T(8,128)(2,1)S(1)} %bitcast.89, bf16[4,256,256]{2,1,0:T(8,128)(2,1)S(1)} %bitcast.91, ...), custom_call_target="tpu_custom_call" | custom-call | flops 3758096384 | bytes 13212057 | tf_op jit(solution)/shard_map/gradient/pallas_call | solution.py:79
  111.7 1.0 slice.38
  112.9 1.0 slice.39
  113.9 2.8 %collective-permute-start.24 = (bf16[2,4,2,32,256]{4,3,2,1,0:T(8,128)(2,1)S(1)}, bf16[2,4,2,32,256]{4,3,2,1,0:T(8,128)(2,1)S(1)}, u32[]{:S(2)}, u32[]{:S(2)}) collective-permute-start(bf16[2,4,2,32,256]{4,3,2,1,0:T(8,128)(2,1)S(1)} %slice.39), channel_id=1, source_target_pairs={{0,7},{1,0},{2,1},{3,2},{4,3},{5,4},{6,5},{7,6},{8,15},{9,8},{10,9... | collective-permute-start | bytes 786440 | tf_op jit(solution)/shard_map/ppermute | solution.py:17
  116.7 1.6 pad_maximum_fusion
  118.3 0.9 collective-permute-done.23
  119.2 0.8 collective-permute-done.24
  120.1 3.6 %gradient.3 = (f32[640,256]{1,0:T(8,128)S(1)}, f32[640,256]{1,0:T(8,128)S(1)}, bf16[32,2,20,256]{3,2,1,0:T(8,128)(2,1)S(1)}) custom-call(s32[4]{0:T(128)S(1)} %copy-done.12, bf16[4,512,384]{2,1,0:T(8,128)(2,1)S(1)} %bitcast.87, bf16[4,256,256]{2,1,0:T(8,128)(2,1)} %bitcast.34.refs_2_, ...), custom_call_target="tpu_custom_call", output_to_operand_aliasing={{0}: (6, {}), {1}: (7, {})} | custom-call | flops 1610612736 | bytes 5662310 | tf_op jit(solution)/shard_map/gradient/pallas_call | solution.py:79
  123.7 0.8 copy-done.6
  124.5 1.3 copy.48
  125.9 8.1 %all-to-all-start.1 = ((bf16[32,2,20,256]{3,1,2,0:T(2,128)(2,1)}), bf16[32,2,20,256]{3,1,2,0:T(2,128)(2,1)S(1)}, u32[]{:S(2)}, u32[]{:S(2)}) async-start(bf16[32,2,20,256]{3,1,2,0:T(2,128)(2,1)} %copy.48), calls=%async_computation.1 | async-start | bytes 1310720 | tf_op jit(solution)/shard_map/all_to_all | solution.py:147
  134.1 9.4 %collective-permute-done.25 = f32[640,256]{1,0:T(8,128)S(1)} collective-permute-done((f32[640,256]{1,0:T(8,128)S(1)}, f32[640,256]{1,0:T(8,128)S(1)}, u32[]{:S(2)}, u32[]{:S(2)}) %collective-permute-start.25) | collective-permute-done | bytes 655392 | tf_op jit(solution)/shard_map/ppermute | solution.py:17
  143.7 3.5 %all-to-all-done.1 = bf16[32,2,20,256]{3,1,2,0:T(2,128)(2,1)S(1)} async-done(((bf16[32,2,20,256]{3,1,2,0:T(2,128)(2,1)}), bf16[32,2,20,256]{3,1,2,0:T(2,128)(2,1)S(1)}, u32[]{:S(2)}, u32[]{:S(2)}) %all-to-all-start.1) | async-done | bytes 655392 | tf_op jit(solution)/shard_map/all_to_all | solution.py:147
  147.9 8.5 %collective-permute-start.26 = (bf16[20,16384]{1,0:T(8,128)(2,1)S(1)}, bf16[20,16384]{1,0:T(8,128)(2,1)}, u32[]{:S(2)}, u32[]{:S(2)}) collective-permute-start(bf16[20,16384]{1,0:T(8,128)(2,1)S(1)} %bitcast.104), channel_id=1, source_target_pairs={{0,64},{64,0},{1,65},{65,1},{2,66},{66,2},{3,67},{67,3},{4,68},{68... | collective-permute-start | bytes 1966088 | tf_op jit(solution)/shard_map/ppermute | solution.py:17
  156.5 3.3 %collective-permute-start.27 = (bf16[20,16384]{1,0:T(8,128)(2,1)S(1)}, bf16[20,16384]{1,0:T(8,128)(2,1)S(1)}, u32[]{:S(2)}, u32[]{:S(2)}) collective-permute-start(bf16[20,16384]{1,0:T(8,128)(2,1)S(1)} %bitcast.105), channel_id=1, source_target_pairs={{0,128},{128,0},{1,129},{129,1},{2,130},{130,2},{3,131},{131,3},{4... | collective-permute-start | bytes 1966088 | tf_op jit(solution)/shard_map/ppermute | solution.py:17
  159.8 2.0 fusion.6
  162.2 21.0 %collective-permute-done.27 = bf16[20,16384]{1,0:T(8,128)(2,1)S(1)} collective-permute-done((bf16[20,16384]{1,0:T(8,128)(2,1)S(1)}, bf16[20,16384]{1,0:T(8,128)(2,1)S(1)}, u32[]{:S(2)}, u32[]{:S(2)}) %collective-permute-start.27) | collective-permute-done | bytes 655392 | tf_op jit(solution)/shard_map/ppermute | solution.py:17
  183.2 1.8 collective-permute-start.28
  185.0 1.8 maximum_select_fusion.1
  187.9 3.5 %copy.50 = bf16[4,20,16384]{2,0,1:T(4,128)(2,1)} copy(bf16[4,20,16384]{2,1,0:T(8,128)(2,1)S(1)} %bitcast.96) | data formatting | bytes 5242880
  191.4 2.1 %all-gather.5.cloned.1.call-done = bf16[5120,256]{1,0:T(8,128)(2,1)} async-done(((bf16[1280,256]{1,0:T(8,128)(2,1)}), bf16[5120,256]{1,0:T(8,128)(2,1)}) %all-gather.5.cloned.1.call-update) | async-done | bytes 2621456 | tf_op jit(solution)/shard_map/all_gather | solution.py:159
  193.5 3.4 %copy.68 = bf16[5120,256]{1,0:T(8,128)(2,1)} copy(bf16[5120,256]{1,0:T(8,128)(2,1)} %all-gather.5.cloned.1.call-done) | data formatting | bytes 5242880
  (74 shorter events, 6.5 us)
Async XLA Ops:
  7.2 91.6 %all-gather.3.cloned.1.call-start = ((), (), s32[]{:S(2)}) async-start(), calls=%async_computation.2 | async-start | bytes 9437184 | tf_op jit(solution)/shard_map/all_gather | solution.py:109
  23.1 9.4 %collective-permute-start.2 = (bf16[8,32,256]{2,1,0:T(8,128)(2,1)S(1)}, bf16[8,32,256]{2,1,0:T(8,128)(2,1)S(1)}, u32[]{:S(2)}, u32[]{:S(2)}) collective-permute-start(bf16[8,32,256]{2,1,0:T(8,128)(2,1)S(1)} %slice.41), channel_id=1, source_target_pairs={{0,16},{16,32},{32,48},{48,0},{1,17},{17,33},{33,49},{49,1},{2,18}... | collective-permute-start | bytes 393224 | tf_op jit(solution)/shard_map/ppermute | solution.py:17
  24.5 8.0 %collective-permute-start.3 = (bf16[8,32,256]{2,1,0:T(8,128)(2,1)S(1)}, bf16[8,32,256]{2,1,0:T(8,128)(2,1)S(1)}, u32[]{:S(2)}, u32[]{:S(2)}) collective-permute-start(bf16[8,32,256]{2,1,0:T(8,128)(2,1)S(1)} %slice.41), channel_id=1, source_target_pairs={{0,48},{16,0},{32,16},{48,32},{1,49},{17,1},{33,17},{49,33},{2,50}... | collective-permute-start | bytes 393224 | tf_op jit(solution)/shard_map/ppermute | solution.py:17
  26.0 9.8 %collective-permute-start = (bf16[8,32,384]{2,1,0:T(8,128)(2,1)S(1)}, bf16[8,32,384]{2,1,0:T(8,128)(2,1)S(1)}, u32[]{:S(2)}, u32[]{:S(2)}) collective-permute-start(bf16[8,32,384]{2,1,0:T(8,128)(2,1)S(1)} %slice.40), channel_id=1, source_target_pairs={{0,1},{1,2},{2,3},{3,4},{4,5},{5,6},{6,7},{7,0},{8,9},{9,10},{10,1... | collective-permute-start | bytes 589832 | tf_op jit(solution)/shard_map/ppermute | solution.py:17
  27.8 8.1 %collective-permute-start.1 = (bf16[8,32,384]{2,1,0:T(8,128)(2,1)S(1)}, bf16[8,32,384]{2,1,0:T(8,128)(2,1)S(1)}, u32[]{:S(2)}, u32[]{:S(2)}) collective-permute-start(bf16[8,32,384]{2,1,0:T(8,128)(2,1)S(1)} %slice.40), channel_id=1, source_target_pairs={{0,7},{1,0},{2,1},{3,2},{4,3},{5,4},{6,5},{7,6},{8,15},{9,8},{10,9... | collective-permute-start | bytes 589832 | tf_op jit(solution)/shard_map/ppermute | solution.py:17
  35.9 7.4 %collective-permute-start.4 = (bf16[8,32,384]{2,1,0:T(8,128)(2,1)S(1)}, bf16[8,32,384]{2,1,0:T(8,128)(2,1)S(1)}, u32[]{:S(2)}, u32[]{:S(2)}) collective-permute-start(bf16[8,32,384]{2,1,0:T(8,128)(2,1)S(1)} %collective-permute-done), channel_id=1, source_target_pairs={{0,1},{1,2},{2,3},{3,4},{4,5},{5,6},{6,7},{7,0},{8,9},{9,10},{10,1... | collective-permute-start | bytes 589832 | tf_op jit(solution)/shard_map/ppermute | solution.py:17
  35.9 7.4 %collective-permute-start.5 = (bf16[8,32,384]{2,1,0:T(8,128)(2,1)S(1)}, bf16[8,32,384]{2,1,0:T(8,128)(2,1)S(1)}, u32[]{:S(2)}, u32[]{:S(2)}) collective-permute-start(bf16[8,32,384]{2,1,0:T(8,128)(2,1)S(1)} %collective-permute-done.1), channel_id=1, source_target_pairs={{0,7},{1,0},{2,1},{3,2},{4,3},{5,4},{6,5},{7,6},{8,15},{9,8},{10,9... | collective-permute-start | bytes 589832 | tf_op jit(solution)/shard_map/ppermute | solution.py:17
  38.6 4.7 %collective-permute-start.6 = (bf16[8,16,256]{2,1,0:T(8,128)(2,1)S(1)}, bf16[8,16,256]{2,1,0:T(8,128)(2,1)S(1)}, u32[]{:S(2)}, u32[]{:S(2)}) collective-permute-start(bf16[8,16,256]{2,1,0:T(8,128)(2,1)S(1)} %slice.32), channel_id=1, source_target_pairs={{0,16},{16,32},{32,48},{48,0},{1,17},{17,33},{33,49},{49,1},{2,18}... | collective-permute-start | bytes 196616 | tf_op jit(solution)/shard_map/ppermute | solution.py:17
  38.6 4.7 %collective-permute-start.7 = (bf16[8,16,256]{2,1,0:T(8,128)(2,1)S(1)}, bf16[8,16,256]{2,1,0:T(8,128)(2,1)S(1)}, u32[]{:S(2)}, u32[]{:S(2)}) collective-permute-start(bf16[8,16,256]{2,1,0:T(8,128)(2,1)S(1)} %slice.33), channel_id=1, source_target_pairs={{0,48},{16,0},{32,16},{48,32},{1,49},{17,1},{33,17},{49,33},{2,50}... | collective-permute-start | bytes 196616 | tf_op jit(solution)/shard_map/ppermute | solution.py:17
  43.3 6.2 %collective-permute-start.8 = (bf16[8,32,384]{2,1,0:T(8,128)(2,1)S(1)}, bf16[8,32,384]{2,1,0:T(8,128)(2,1)S(1)}, u32[]{:S(2)}, u32[]{:S(2)}) collective-permute-start(bf16[8,32,384]{2,1,0:T(8,128)(2,1)S(1)} %collective-permute-done.4), channel_id=1, source_target_pairs={{0,1},{1,2},{2,3},{3,4},{4,5},{5,6},{6,7},{7,0},{8,9},{9,10},{10,1... | collective-permute-start | bytes 589832 | tf_op jit(solution)/shard_map/ppermute | solution.py:17
  43.6 5.9 %collective-permute-start.9 = (bf16[8,32,384]{2,1,0:T(8,128)(2,1)S(1)}, bf16[8,32,384]{2,1,0:T(8,128)(2,1)S(1)}, u32[]{:S(2)}, u32[]{:S(2)}) collective-permute-start(bf16[8,32,384]{2,1,0:T(8,128)(2,1)S(1)} %collective-permute-done.5), channel_id=1, source_target_pairs={{0,7},{1,0},{2,1},{3,2},{4,3},{5,4},{6,5},{7,6},{8,15},{9,8},{10,9... | collective-permute-start | bytes 589832 | tf_op jit(solution)/shard_map/ppermute | solution.py:17
  46.1 18.1 %copy-start.2 = (bf16[4,4,2,32,256]{4,3,2,1,0:T(8,128)(2,1)}, bf16[4,4,2,32,256]{4,3,2,1,0:T(8,128)(2,1)S(1)}, u32[]{:S(2)}) copy-start(bf16[4,4,2,32,256]{4,3,2,1,0:T(8,128)(2,1)S(1)} %pad_maximum_fusion.1) | copy-start | bytes 1572868
  49.5 5.2 %collective-permute-start.10 = (bf16[8,16,384]{2,1,0:T(8,128)(2,1)S(1)}, bf16[8,16,384]{2,1,0:T(8,128)(2,1)S(1)}, u32[]{:S(2)}, u32[]{:S(2)}) collective-permute-start(bf16[8,16,384]{2,1,0:T(8,128)(2,1)S(1)} %slice.34), channel_id=1, source_target_pairs={{0,1},{1,2},{2,3},{3,4},{4,5},{5,6},{6,7},{7,0},{8,9},{9,10},{10,1... | collective-permute-start | bytes 294920 | tf_op jit(solution)/shard_map/ppermute | solution.py:17
  50.1 4.6 %collective-permute-start.11 = (bf16[8,16,384]{2,1,0:T(8,128)(2,1)S(1)}, bf16[8,16,384]{2,1,0:T(8,128)(2,1)S(1)}, u32[]{:S(2)}, u32[]{:S(2)}) collective-permute-start(bf16[8,16,384]{2,1,0:T(8,128)(2,1)S(1)} %slice.35), channel_id=1, source_target_pairs={{0,7},{1,0},{2,1},{3,2},{4,3},{5,4},{6,5},{7,6},{8,15},{9,8},{10,9... | collective-permute-start | bytes 294920 | tf_op jit(solution)/shard_map/ppermute | solution.py:17
  57.5 32.7 %collective-permute-start.12 = (bf16[8,8,32,384]{3,2,1,0:T(8,128)(2,1)}, bf16[8,8,32,384]{3,2,1,0:T(8,128)(2,1)S(1)}, u32[]{:S(2)}, u32[]{:S(2)}) collective-permute-start(bf16[8,8,32,384]{3,2,1,0:T(8,128)(2,1)} %bitcast_dynamic-update-slice_fusion.6), channel_id=1, source_target_pairs={{0,16},{16,32},{32,48},{48,0},{1,17},{17,33},{33,49},{49,1},{2,18}... | collective-permute-start | bytes 4718600 | tf_op jit(solution)/shard_map/ppermute | solution.py:17
  57.5 32.7 %collective-permute-start.13 = (bf16[8,8,32,384]{3,2,1,0:T(8,128)(2,1)}, bf16[8,8,32,384]{3,2,1,0:T(8,128)(2,1)}, u32[]{:S(2)}, u32[]{:S(2)}) collective-permute-start(bf16[8,8,32,384]{3,2,1,0:T(8,128)(2,1)} %bitcast_dynamic-update-slice_fusion.6), channel_id=1, source_target_pairs={{0,48},{16,0},{32,16},{48,32},{1,49},{17,1},{33,17},{49,33},{2,50}... | collective-permute-start | bytes 4718600 | tf_op jit(solution)/shard_map/ppermute | solution.py:17
  62.1 25.2 %collective-permute-start.14 = (f32[2,4,160,256]{3,2,1,0:T(8,128)S(1)}, f32[2,4,160,256]{3,2,1,0:T(8,128)S(1)}, u32[]{:S(2)}, u32[]{:S(2)}) collective-permute-start(f32[2,4,160,256]{3,2,1,0:T(8,128)S(1)} %get-tuple-element.39), channel_id=1, source_target_pairs={{0,8},{8,0},{1,9},{9,1},{2,10},{10,2},{3,11},{11,3},{4,12},{12,4},... | collective-permute-start | bytes 3932168 | tf_op jit(solution)/shard_map/ppermute | solution.py:17
  62.2 9.7 %collective-permute-start.17 = (bf16[4,4,2,32,256]{4,3,2,1,0:T(8,128)(2,1)S(1)}, bf16[4,4,2,32,256]{4,3,2,1,0:T(8,128)(2,1)S(1)}, u32[]{:S(2)}, u32[]{:S(2)}) collective-permute-start(bf16[4,4,2,32,256]{4,3,2,1,0:T(8,128)(2,1)S(1)} %pad_maximum_fusion.1), channel_id=1, source_target_pairs={{0,1},{1,2},{2,3},{3,4},{4,5},{5,6},{6,7},{7,0},{8,9},{9,10},{10,1... | collective-permute-start | bytes 1572872 | tf_op jit(solution)/shard_map/ppermute | solution.py:17
  64.2 9.2 %collective-permute-start.20 = (bf16[4,4,2,32,256]{4,3,2,1,0:T(8,128)(2,1)S(1)}, bf16[4,4,2,32,256]{4,3,2,1,0:T(8,128)(2,1)S(1)}, u32[]{:S(2)}, u32[]{:S(2)}) collective-permute-start(bf16[4,4,2,32,256]{4,3,2,1,0:T(8,128)(2,1)S(1)} %pad_maximum_fusion.1), channel_id=1, source_target_pairs={{0,7},{1,0},{2,1},{3,2},{4,3},{5,4},{6,5},{7,6},{8,15},{9,8},{10,9... | collective-permute-start | bytes 1572872 | tf_op jit(solution)/shard_map/ppermute | solution.py:17
  71.9 24.0 %collective-permute-start.18 = (bf16[4,4,2,32,256]{4,3,2,1,0:T(8,128)(2,1)S(1)}, bf16[4,4,2,32,256]{4,3,2,1,0:T(8,128)(2,1)}, u32[]{:S(2)}, u32[]{:S(2)}) collective-permute-start(bf16[4,4,2,32,256]{4,3,2,1,0:T(8,128)(2,1)S(1)} %collective-permute-done.17), channel_id=1, source_target_pairs={{0,1},{1,2},{2,3},{3,4},{4,5},{5,6},{6,7},{7,0},{8,9},{9,10},{10,1... | collective-permute-start | bytes 1572872 | tf_op jit(solution)/shard_map/ppermute | solution.py:17
  72.7 0.8 copy-start.8
  73.5 24.0 %collective-permute-start.21 = (bf16[4,4,2,32,256]{4,3,2,1,0:T(8,128)(2,1)S(1)}, bf16[4,4,2,32,256]{4,3,2,1,0:T(8,128)(2,1)}, u32[]{:S(2)}, u32[]{:S(2)}) collective-permute-start(bf16[4,4,2,32,256]{4,3,2,1,0:T(8,128)(2,1)S(1)} %collective-permute-done.20), channel_id=1, source_target_pairs={{0,7},{1,0},{2,1},{3,2},{4,3},{5,4},{6,5},{7,6},{8,15},{9,8},{10,9... | collective-permute-start | bytes 1572872 | tf_op jit(solution)/shard_map/ppermute | solution.py:17
  75.4 0.8 copy-start.10
  87.3 1.1 copy-start.4
  90.2 8.6 %copy-start.12 = (s32[4]{0:T(128)S(1)}, s32[4]{0:T(128)}, u32[]{:S(2)}) copy-start(s32[4]{0:T(128)} %refs_0_.3) | copy-start | bytes 52
  91.2 25.5 %collective-permute-start.15 = (bf16[4,8,32,384]{3,2,1,0:T(8,128)(2,1)}, bf16[4,8,32,384]{3,2,1,0:T(8,128)(2,1)}, u32[]{:S(2)}, u32[]{:S(2)}) collective-permute-start(bf16[4,8,32,384]{3,2,1,0:T(8,128)(2,1)} %slice.36), channel_id=1, source_target_pairs={{0,16},{16,32},{32,48},{48,0},{1,17},{17,33},{33,49},{49,1},{2,18}... | collective-permute-start | bytes 2359304 | tf_op jit(solution)/shard_map/ppermute | solution.py:17
  93.8 22.9 %collective-permute-start.16 = (bf16[4,8,32,384]{3,2,1,0:T(8,128)(2,1)}, bf16[4,8,32,384]{3,2,1,0:T(8,128)(2,1)}, u32[]{:S(2)}, u32[]{:S(2)}) collective-permute-start(bf16[4,8,32,384]{3,2,1,0:T(8,128)(2,1)} %slice.37), channel_id=1, source_target_pairs={{0,48},{16,0},{32,16},{48,32},{1,49},{17,1},{33,17},{49,33},{2,50}... | collective-permute-start | bytes 2359304 | tf_op jit(solution)/shard_map/ppermute | solution.py:17
  96.0 15.7 %collective-permute-start.19 = (bf16[4,4,2,32,256]{4,3,2,1,0:T(8,128)(2,1)}, bf16[4,4,2,32,256]{4,3,2,1,0:T(8,128)(2,1)}, u32[]{:S(2)}, u32[]{:S(2)}) collective-permute-start(bf16[4,4,2,32,256]{4,3,2,1,0:T(8,128)(2,1)} %collective-permute-done.18), channel_id=1, source_target_pairs={{0,1},{1,2},{2,3},{3,4},{4,5},{5,6},{6,7},{7,0},{8,9},{9,10},{10,1... | collective-permute-start | bytes 1572872 | tf_op jit(solution)/shard_map/ppermute | solution.py:17
  97.5 14.2 %collective-permute-start.22 = (bf16[4,4,2,32,256]{4,3,2,1,0:T(8,128)(2,1)}, bf16[4,4,2,32,256]{4,3,2,1,0:T(8,128)(2,1)}, u32[]{:S(2)}, u32[]{:S(2)}) collective-permute-start(bf16[4,4,2,32,256]{4,3,2,1,0:T(8,128)(2,1)} %collective-permute-done.21), channel_id=1, source_target_pairs={{0,7},{1,0},{2,1},{3,2},{4,3},{5,4},{6,5},{7,6},{8,15},{9,8},{10,9... | collective-permute-start | bytes 1572872 | tf_op jit(solution)/shard_map/ppermute | solution.py:17
  98.8 3.4 %copy-start = (bf16[16384,256]{1,0:T(8,128)(2,1)S(1)}, bf16[16384,256]{1,0:T(8,128)(2,1)}, u32[]{:S(2)}) copy-start(bf16[16384,256]{1,0:T(8,128)(2,1)} %all-gather.3.cloned.1.call-done) | copy-start | bytes 25165828
  102.1 1.0 copy-start.3
  103.2 1.0 copy-start.9
  104.2 1.0 copy-start.11
  105.3 14.8 %copy-start.1 = (bf16[16384,256]{1,0:T(8,128)(2,1)S(1)}, bf16[16384,256]{1,0:T(8,128)(2,1)}, u32[]{:S(2)}) copy-start(bf16[16384,256]{1,0:T(8,128)(2,1)} %all-gather.3.cloned.1.call-done) | copy-start | bytes 25165828
  112.7 6.5 %collective-permute-start.23 = (bf16[2,4,2,32,256]{4,3,2,1,0:T(8,128)(2,1)S(1)}, bf16[2,4,2,32,256]{4,3,2,1,0:T(8,128)(2,1)S(1)}, u32[]{:S(2)}, u32[]{:S(2)}) collective-permute-start(bf16[2,4,2,32,256]{4,3,2,1,0:T(8,128)(2,1)S(1)} %slice.38), channel_id=1, source_target_pairs={{0,1},{1,2},{2,3},{3,4},{4,5},{5,6},{6,7},{7,0},{8,9},{9,10},{10,1... | collective-permute-start | bytes 786440 | tf_op jit(solution)/shard_map/ppermute | solution.py:17
  113.9 6.2 %copy-start.5 = (f32[2,4,160,256]{3,2,1,0:T(8,128)S(1)}, f32[2,4,160,256]{3,2,1,0:T(8,128)}, u32[]{:S(2)}) copy-start(f32[2,4,160,256]{3,2,1,0:T(8,128)} %copy-done.4) | copy-start | bytes 3932164
  113.9 6.1 %collective-permute-start.24 = (bf16[2,4,2,32,256]{4,3,2,1,0:T(8,128)(2,1)S(1)}, bf16[2,4,2,32,256]{4,3,2,1,0:T(8,128)(2,1)S(1)}, u32[]{:S(2)}, u32[]{:S(2)}) collective-permute-start(bf16[2,4,2,32,256]{4,3,2,1,0:T(8,128)(2,1)S(1)} %slice.39), channel_id=1, source_target_pairs={{0,7},{1,0},{2,1},{3,2},{4,3},{5,4},{6,5},{7,6},{8,15},{9,8},{10,9... | collective-permute-start | bytes 786440 | tf_op jit(solution)/shard_map/ppermute | solution.py:17
  123.7 0.8 copy-start.6
  124.5 9.5 %copy-start.7 = (f32[640,256]{1,0:T(8,128)S(1)}, f32[640,256]{1,0:T(8,128)}, u32[]{:S(2)}) copy-start(f32[640,256]{1,0:T(8,128)} %copy-done.6) | copy-start | bytes 1966084
  125.9 21.4 %all-to-all-start.1 = ((bf16[32,2,20,256]{3,1,2,0:T(2,128)(2,1)}), bf16[32,2,20,256]{3,1,2,0:T(2,128)(2,1)S(1)}, u32[]{:S(2)}, u32[]{:S(2)}) async-start(bf16[32,2,20,256]{3,1,2,0:T(2,128)(2,1)} %copy.48), calls=%async_computation.1 | async-start | bytes 1310720 | tf_op jit(solution)/shard_map/all_to_all | solution.py:147
  134.0 59.6 %all-gather.5.cloned.1.call-start = ((), (), s32[]{:S(2)}) async-start(), calls=%async_computation.3 | async-start | bytes 3276800 | tf_op jit(solution)/shard_map/all_gather | solution.py:159
  134.0 9.5 %collective-permute-start.25 = (f32[640,256]{1,0:T(8,128)S(1)}, f32[640,256]{1,0:T(8,128)S(1)}, u32[]{:S(2)}, u32[]{:S(2)}) collective-permute-start(f32[640,256]{1,0:T(8,128)S(1)} %copy-done.7), channel_id=1, source_target_pairs={{0,8},{8,0},{1,9},{9,1},{2,10},{10,2},{3,11},{11,3},{4,12},{12,4},... | collective-permute-start | bytes 1966088 | tf_op jit(solution)/shard_map/ppermute | solution.py:17
  147.4 12.4 %copy-start.13 = (f32[1280,256]{1,0:T(8,128)S(1)}, f32[1280,256]{1,0:T(8,128)}, u32[]{:S(2)}) copy-start(f32[1280,256]{1,0:T(8,128)} %param.8) | copy-start | bytes 3932164
  147.4 12.4 %copy-start.14 = (f32[1280,256]{1,0:T(8,128)S(1)}, f32[1280,256]{1,0:T(8,128)}, u32[]{:S(2)}) copy-start(f32[1280,256]{1,0:T(8,128)} %param.9) | copy-start | bytes 3932164
  147.9 37.1 %collective-permute-start.26 = (bf16[20,16384]{1,0:T(8,128)(2,1)S(1)}, bf16[20,16384]{1,0:T(8,128)(2,1)}, u32[]{:S(2)}, u32[]{:S(2)}) collective-permute-start(bf16[20,16384]{1,0:T(8,128)(2,1)S(1)} %bitcast.104), channel_id=1, source_target_pairs={{0,64},{64,0},{1,65},{65,1},{2,66},{66,2},{3,67},{67,3},{4,68},{68... | collective-permute-start | bytes 1966088 | tf_op jit(solution)/shard_map/ppermute | solution.py:17
  156.5 26.7 %collective-permute-start.27 = (bf16[20,16384]{1,0:T(8,128)(2,1)S(1)}, bf16[20,16384]{1,0:T(8,128)(2,1)S(1)}, u32[]{:S(2)}, u32[]{:S(2)}) collective-permute-start(bf16[20,16384]{1,0:T(8,128)(2,1)S(1)} %bitcast.105), channel_id=1, source_target_pairs={{0,128},{128,0},{1,129},{129,1},{2,130},{130,2},{3,131},{131,3},{4... | collective-permute-start | bytes 1966088 | tf_op jit(solution)/shard_map/ppermute | solution.py:17
  183.2 3.7 %collective-permute-start.28 = (bf16[20,16384]{1,0:T(8,128)(2,1)S(1)}, bf16[20,16384]{1,0:T(8,128)(2,1)S(1)}, u32[]{:S(2)}, u32[]{:S(2)}) collective-permute-start(bf16[20,16384]{1,0:T(8,128)(2,1)S(1)} %collective-permute-done.27), channel_id=1, source_target_pairs={{0,64},{64,0},{1,65},{65,1},{2,66},{66,2},{3,67},{67,3},{4,68},{68... | collective-permute-start | bytes 1966088 | tf_op jit(solution)/shard_map/ppermute | solution.py:17
Sparse Core Ops, SparseCore 0:
  9.9 56.4 all-gather.2
  161.9 31.5 all-gather.4
